TPU v7x, 32 devices: a whole 2x2x4 slice. The times are simulated.
32 devices in a mesh: leaf: 4 (over z), row: 2 (over y), col: 4 (over x, core).
Axes of the slice: x: 2, y: 2, z: 4, core: 2. Of those that a mesh axis runs over, the one named last changes fastest.
Arguments:
- rhs_root: bfloat16 [64, 4, 768], P('col', None, ('leaf', 'row')), may hold values from -6 to 6
- rhs_child: bfloat16 [64, 4, 768], P('col', None, ('leaf', 'row')), may hold values from -6 to 6
- subtree_update: bfloat16 [64, 4, 1024], P('col', None, ('leaf', 'row')), may hold values from -6 to 6
- inv_root: bfloat16 [4, 768, 3072], P(None, ('leaf', 'row'), 'col'), as said below
- inv_child: bfloat16 [4, 768, 1536], P(None, ('leaf', 'row'), 'col'), as said below
- off_child: bfloat16 [4, 1024, 1536], P(None, ('leaf', 'row'), 'col'), may hold values from -0.15625 to 0.15625
- child_map: int32 [2, 16], replicated, may hold values from 0 to 23, as said below
- subtree_map: int32 [4, 8], replicated, may hold values from 0 to 27, as said below
Outputs:
- solution_root: float32 [64, 4, 768], P('col', None, ('leaf', 'row'))
- solution_child: float32 [64, 4, 768], P('col', None, ('leaf', 'row'))
- leaf_solution: bfloat16 [64, 4, 1024], P('col', None, ('leaf', 'row'))
Inputs may be any that keep to these rules, and one draw needn't show every extreme that they name: `child_map`: each row names 16 different blocks. `subtree_map`: each row names 8 different blocks. `inv_root`: zero above the diagonal, positive on it. `inv_child`: each child's block is zero above the diagonal, positive on it.
All inputs are finite; a program needn't handle non-finite values.
Results may differ from a plain program's by a relative error of at most 0.017.
Values may be sent and summed in bfloat16 or wider, within the bound.
A program may use at most 64 MiB of HBM per device.

v0:
```python
import jax
import jax.numpy as jnp
from jax import lax
from jax.sharding import PartitionSpec as P

BLOCK_ROWS = 128


def partner_2(block, axis, bit):
    count = lax.axis_size(axis)
    route = []
    for low in range(count):
        high = low | 1 << bit
        if high != low and high < count:
            route += [(low, high), (high, low)]
    return lax.ppermute(block, axis, route)


def group_gather(piece, group_size):
    merged = lax.all_gather(piece, "row", axis=2, tiled=True)
    leaf_index = lax.axis_index("leaf")
    for bit_number in range(group_size.bit_length() - 1):
        partner = partner_2(merged, "leaf", bit_number)
        upper = leaf_index >> bit_number & 1 == 1
        merged = jnp.where(
            upper, jnp.concatenate([partner, merged], 2), jnp.concatenate([merged, partner], 2)
        )
    return merged


def group_sum(partial_sum, group_size):
    leaf_index = lax.axis_index("leaf")
    for bit_number in reversed(range(group_size.bit_length() - 1)):
        middle = partial_sum.shape[1] // 2
        lower_half = partial_sum[:, :middle]
        upper_half = partial_sum[:, middle:]
        upper = leaf_index >> bit_number & 1 == 1
        outgoing = jnp.where(upper, lower_half, upper_half)
        kept_half = jnp.where(upper, upper_half, lower_half)
        partial_sum = kept_half + partner_2(
            outgoing.astype(jnp.bfloat16), "leaf", bit_number
        ).astype(outgoing.dtype)
    return lax.psum_scatter(
        partial_sum.astype(jnp.bfloat16), "row", scatter_dimension=1, tiled=True
    ).astype(jnp.float32)


def one_hot(block_map, blocks_total):
    return (block_map[..., None] == jnp.arange(blocks_total, dtype=jnp.int32)).astype(jnp.bfloat16)


def pick_piece(source, position, along):
    return lax.dynamic_index_in_dim(source, position, along, keepdims=False)


def contract(left_side, right_side, left_dim, right_dim):
    return lax.dot_general(
        left_side,
        right_side,
        (((left_dim,), (right_dim,)), ((), ())),
        preferred_element_type=jnp.float32,
    )


def local(
    rhs_root, rhs_child, subtree_update, inv_root, inv_child, off_child, child_map, subtree_map
):
    n_col = lax.axis_size("col")
    n_row = lax.axis_size("row")
    n_leaf = lax.axis_size("leaf")
    group_size = n_leaf // 2
    sub_size = n_leaf // 4
    col_index = lax.axis_index("col")
    leaf_index = lax.axis_index("leaf")
    row_index = lax.axis_index("row")
    front_index = leaf_index // group_size
    member = leaf_index % group_size
    child_rank = member * n_row + row_index
    half_index = member // sub_size
    sub_rank = member % sub_size * n_row + row_index
    panel_width = rhs_child.shape[0]
    right_sides = panel_width * n_col
    sep_piece = rhs_child.shape[2]
    upd_piece = subtree_update.shape[2]
    root_width = inv_root.shape[2]
    child_width = inv_child.shape[2]
    child_order = child_width * n_col
    child_update = upd_piece * n_col * group_size * n_row
    root_blocks = root_width * n_col // BLOCK_ROWS
    child_blocks = (child_order + child_update) // BLOCK_ROWS
    root_matrix = inv_root.reshape(n_col * sep_piece, root_width)
    child_matrix = inv_child.reshape(n_col * sep_piece, child_width)
    off_matrix = off_child.reshape(n_col * upd_piece, child_width)
    joined = jnp.concatenate([subtree_update, rhs_child], 2)
    gathered = group_gather(joined, group_size).reshape(
        panel_width, n_col, group_size * n_row, upd_piece + sep_piece
    )
    sub_vectors = (
        gathered[..., :upd_piece]
        .reshape(panel_width, n_col, 2, -1)
        .transpose(2, 0, 1, 3)
        .reshape(2, panel_width, -1, BLOCK_ROWS)
    )
    child_rhs_full = gathered[..., upd_piece:].reshape(panel_width, child_order)
    sub_rows = lax.dynamic_slice_in_dim(subtree_map, 2 * front_index, 2, 0)
    spread = jnp.einsum(
        "hpjt,hjn->pnt",
        sub_vectors,
        one_hot(sub_rows, child_blocks),
        preferred_element_type=jnp.float32,
    ).reshape(panel_width, -1)
    child_sep = (spread[:, :child_order] + child_rhs_full.astype(jnp.float32)).astype(jnp.bfloat16)
    child_tail = spread[:, child_order:]
    child_tile = lax.all_to_all(
        child_sep.reshape(panel_width, n_col, child_width),
        "col",
        split_axis=1,
        concat_axis=0,
        tiled=True,
    ).reshape(right_sides, child_width)
    child_forward = lax.psum(contract(child_tile, child_matrix, 1, 1), "col").astype(jnp.bfloat16)
    forward_quarter = lax.dynamic_slice_in_dim(
        child_forward.reshape(right_sides, n_col, sep_piece), col_index, 1, 1
    )
    forward_tile = group_gather(forward_quarter, group_size).reshape(right_sides, child_width)
    pass_term = lax.psum_scatter(
        contract(forward_tile, off_matrix, 1, 1), "col", scatter_dimension=0, tiled=True
    )
    tail_mine = pick_piece(
        child_tail.reshape(panel_width, n_col, group_size * n_row, upd_piece), child_rank, 2
    )
    child_pass = (tail_mine - pass_term.reshape(panel_width, n_col, upd_piece)).astype(jnp.bfloat16)
    joined_root = jnp.concatenate([child_pass, rhs_root], 2)
    root_all = lax.all_gather(joined_root, ("leaf", "row"), axis=2, tiled=True).reshape(
        panel_width, n_col, n_leaf * n_row, upd_piece + sep_piece
    )
    pass_vectors = (
        root_all[..., :upd_piece]
        .reshape(panel_width, n_col, 2, -1)
        .transpose(2, 0, 1, 3)
        .reshape(2, panel_width, -1, BLOCK_ROWS)
    )
    root_rhs_full = root_all[..., upd_piece:].reshape(panel_width, root_width * n_col)
    root_spread = jnp.einsum(
        "hpjt,hjn->pnt",
        pass_vectors,
        one_hot(child_map, root_blocks),
        preferred_element_type=jnp.float32,
    ).reshape(panel_width, -1)
    root_sep = (root_spread + root_rhs_full.astype(jnp.float32)).astype(jnp.bfloat16)
    root_tile = lax.all_to_all(
        root_sep.reshape(panel_width, n_col, root_width),
        "col",
        split_axis=1,
        concat_axis=0,
        tiled=True,
    ).reshape(right_sides, root_width)
    root_forward = lax.psum(contract(root_tile, root_matrix, 1, 1), "col").astype(jnp.bfloat16)
    map_row = pick_piece(child_map, front_index, 0)
    root_piece = lax.psum_scatter(
        contract(root_matrix, root_forward, 0, 1), ("leaf", "row"), scatter_dimension=0, tiled=True
    )
    solution_root = lax.all_to_all(
        root_piece.T.reshape(right_sides, 1, sep_piece),
        "col",
        split_axis=0,
        concat_axis=1,
        tiled=True,
    )
    root_everywhere = lax.all_gather(
        solution_root.astype(jnp.bfloat16), ("leaf", "row"), axis=2, tiled=True
    ).reshape(panel_width, root_blocks, BLOCK_ROWS)
    known_full = (
        jnp.einsum(
            "pnt,jn->pjt",
            root_everywhere,
            one_hot(map_row, root_blocks),
            preferred_element_type=jnp.float32,
        )
        .astype(jnp.bfloat16)
        .reshape(panel_width, child_update)
    )
    known_mine = pick_piece(
        known_full.reshape(panel_width, n_col, group_size * n_row, upd_piece), child_rank, 2
    )
    known_rows = lax.all_gather(known_mine, "col", axis=0, tiled=True).reshape(
        right_sides, n_col * upd_piece
    )
    correction = group_sum(contract(known_rows, off_matrix, 1, 0), group_size)
    back_quarter = (
        forward_quarter.reshape(right_sides, sep_piece).astype(jnp.float32) - correction
    ).astype(jnp.bfloat16)
    back_rows = lax.all_gather(
        back_quarter.reshape(right_sides, 1, sep_piece), "col", axis=1, tiled=True
    ).reshape(right_sides, n_col * sep_piece)
    child_piece = group_sum(contract(back_rows, child_matrix, 1, 0), group_size)
    solution_child = lax.all_to_all(
        child_piece.reshape(right_sides, 1, sep_piece),
        "col",
        split_axis=0,
        concat_axis=1,
        tiled=True,
    )
    child_rounded = solution_child.astype(jnp.bfloat16)
    sep_whole = group_gather(child_rounded, group_size).reshape(panel_width, child_order)
    child_whole = jnp.concatenate([sep_whole, known_full], 1)
    sub_row = pick_piece(subtree_map, 2 * front_index + half_index, 0)
    leaf_full = jnp.einsum(
        "pnt,jn->pjt",
        child_whole.reshape(panel_width, child_blocks, BLOCK_ROWS),
        one_hot(sub_row, child_blocks),
        preferred_element_type=jnp.float32,
    ).astype(jnp.bfloat16)
    leaf_solution = pick_piece(
        leaf_full.reshape(panel_width, n_col, sub_size * n_row, upd_piece), sub_rank, 2
    )
    return (solution_root, solution_child, leaf_solution)


def solution(mesh):
    in_specs = (
        P("col", None, ("leaf", "row")),
        P("col", None, ("leaf", "row")),
        P("col", None, ("leaf", "row")),
        P(None, ("leaf", "row"), "col"),
        P(None, ("leaf", "row"), "col"),
        P(None, ("leaf", "row"), "col"),
        P(),
        P(),
    )
    out_specs = (
        P("col", None, ("leaf", "row")),
        P("col", None, ("leaf", "row")),
        P("col", None, ("leaf", "row")),
    )
    return jax.shard_map(local, mesh=mesh, in_specs=in_specs, out_specs=out_specs, check_vma=False)
```

profile of v0, /device:TPU:0, one launch (start us, length us, event | category | flops | bytes accessed | tf_op | source)
XLA Modules:
  0.0 315.4 jit_solution(6186895764628182573)
XLA Ops:
  7.2 0.9 copy.131
  9.2 9.2 %all_gather.21 = bf16[16,4,448]{0,1,2:T(4,128)(2,1)S(1)} all-gather(bf16[16,4,224]{0,1,2:T(4,128)(2,1)S(1)} %pad_maximum_fusion), channel_id=1, replica_groups=mesh['leaf'=4,'row'=2,'col'=4] {'row'}, dimensions={2}, use_global_device_ids=true | all-gather | bytes 86016 | tf_op jit(solution)/shard_map/all_gather | solution.py:20
  18.4 1.8 collective-permute-start
  20.6 9.6 %collective-permute-done = bf16[16,4,448]{0,1,2:T(4,128)(2,1)S(1)} collective-permute-done((bf16[16,4,448]{0,1,2:T(4,128)(2,1)S(1)}, bf16[16,4,448]{0,1,2:T(4,128)(2,1)S(1)}, u32[]{:S(2)}, u32[]{:S(2)}) %collective-permute-start) | collective-permute-done | bytes 57376 | tf_op jit(solution)/shard_map/ppermute | solution.py:16
  32.2 3.3 %all-to-all-start = ((bf16[16,4,384]{2,0,1:T(8,128)(2,1)}), bf16[16,4,384]{2,0,1:T(8,128)(2,1)S(1)}, u32[]{:S(2)}, u32[]{:S(2)}) async-start(bf16[16,4,384]{2,0,1:T(8,128)(2,1)} %bitcast.141), calls=%async_computation | async-start | bytes 98304 | tf_op jit(solution)/shard_map/all_to_all | solution.py:114
  35.5 3.9 %all-to-all-done = bf16[16,4,384]{2,0,1:T(8,128)(2,1)S(1)} async-done(((bf16[16,4,384]{2,0,1:T(8,128)(2,1)}), bf16[16,4,384]{2,0,1:T(8,128)(2,1)S(1)}, u32[]{:S(2)}, u32[]{:S(2)}) %all-to-all-start) | async-done | bytes 49184 | tf_op jit(solution)/shard_map/all_to_all | solution.py:114
  39.7 11.1 %psum.14 = bf16[64,384]{1,0:T(8,128)(2,1)S(1)} all-reduce(f32[64,384]{1,0:T(8,128)S(1)} %fusion.31), channel_id=1, replica_groups=mesh['leaf'=4,'row'=2,'col'=4] {'col'}, use_global_device_ids=true, to_apply=%region_0.1 | all-reduce | flops 24576 | bytes 147456 | tf_op jit(solution)/shard_map/psum | solution.py:121
  51.1 4.8 %all_gather.22 = bf16[64,1,192]{0,1,2:T(2,128)(2,1)S(1)} all-gather(bf16[64,1,96]{0,1,2:T(2,128)(2,1)S(1)} %copy.178), channel_id=1, replica_groups=mesh['leaf'=4,'row'=2,'col'=4] {'row'}, dimensions={2}, use_global_device_ids=true | all-gather | bytes 36864 | tf_op jit(solution)/shard_map/all_gather | solution.py:20
  55.9 1.6 collective-permute-start.1
  57.5 2.4 collective-permute-done.1
  61.4 20.5 %reduce-scatter.11.cloned.1.call-done = f32[16,512]{1,0:T(8,128)} async-done(((f32[64,512]{1,0:T(8,128)}), f32[16,512]{1,0:T(8,128)}) %reduce-scatter.11.cloned.1.call-update) | async-done | bytes 32784 | tf_op jit(solution)/shard_map/reduce_scatter | solution.py:126
  83.1 41.1 %all_gather.23 = bf16[16,4,1792]{0,1,2:T(4,128)(2,1)S(1)} all-gather(bf16[16,4,224]{0,1,2:T(4,128)(2,1)S(1)} %pad_maximum_fusion.1), channel_id=1, replica_groups=mesh['leaf'=4,'row'=2,'col'=4] {'leaf','row'}, dimensions={2}, use_global_device_ids=true | all-gather | bytes 258048 | tf_op jit(solution)/shard_map/all_gather | solution.py:134
  126.7 6.7 %all_to_all.66 = bf16[16,4,768]{2,0,1:T(8,128)(2,1)S(1)} all-to-all(bf16[16,4,768]{2,0,1:T(8,128)(2,1)S(1)} %fusion.1), channel_id=1, replica_groups=mesh['leaf'=4,'row'=2,'col'=4] {'col'}, dimensions={1} | all-to-all | bytes 196608 | tf_op jit(solution)/shard_map/all_to_all | solution.py:151
  133.7 11.2 %psum.15 = bf16[64,384]{1,0:T(8,128)(2,1)S(1)} all-reduce(f32[64,384]{1,0:T(8,128)S(1)} %fusion.32), channel_id=1, replica_groups=mesh['leaf'=4,'row'=2,'col'=4] {'col'}, use_global_device_ids=true, to_apply=%region_2.3 | all-reduce | flops 24576 | bytes 147456 | tf_op jit(solution)/shard_map/psum | solution.py:158
  145.0 0.9 copy.172
  146.0 60.1 %reduce-scatter.13.cloned.1.call-done = f32[96,64]{1,0:T(8,128)} async-done(((f32[768,64]{1,0:T(8,128)}), f32[96,64]{1,0:T(8,128)}) %reduce-scatter.13.cloned.1.call-update) | async-done | bytes 24592
  206.1 1.5 copy.173
  207.6 3.3 %all-to-all-start.2 = ((f32[64,1,96]{2,1,0:T(1,128)}), f32[64,1,96]{2,1,0:T(1,128)S(1)}, u32[]{:S(2)}, u32[]{:S(2)}) async-start(f32[64,1,96]{2,1,0:T(1,128)} %bitcast.28), calls=%async_computation.3 | async-start | bytes 65536 | tf_op jit(solution)/shard_map/all_to_all | solution.py:163
  211.0 3.8 %all-to-all-done.2 = f32[64,1,96]{2,1,0:T(1,128)S(1)} async-done(((f32[64,1,96]{2,1,0:T(1,128)}), f32[64,1,96]{2,1,0:T(1,128)S(1)}, u32[]{:S(2)}, u32[]{:S(2)}) %all-to-all-start.2) | async-done | bytes 24608 | tf_op jit(solution)/shard_map/all_to_all | solution.py:163
  215.0 32.0 %all_gather.24 = bf16[16,4,768]{0,1,2:T(4,128)(2,1)S(1)} all-gather(bf16[16,4,96]{0,1,2:T(4,128)(2,1)S(1)} %bitcast.161), channel_id=1, replica_groups=mesh['leaf'=4,'row'=2,'col'=4] {'leaf','row'}, dimensions={2}, use_global_device_ids=true | all-gather | bytes 110592 | tf_op jit(solution)/shard_map/all_gather | solution.py:170
  247.8 5.2 %all-gather = bf16[64,4,1,128]{3,0,1,2:T(8,128)(2,1)S(1)} all-gather(bf16[16,4,1,128]{3,0,1,2:T(8,128)(2,1)S(1)} %copy.181), channel_id=2, replica_groups=mesh['leaf'=4,'row'=2,'col'=4] {'col'}, dimensions={0}, use_global_device_ids=true | all-gather | bytes 81920 | tf_op jit(solution)/shard_map/all_gather | solution.py:186
  253.4 3.9 %collective-permute-done.2 = bf16[64,192]{1,0:T(8,128)(2,1)S(1)} collective-permute-done((bf16[64,192]{1,0:T(8,128)(2,1)S(1)}, bf16[64,192]{1,0:T(8,128)(2,1)S(1)}, u32[]{:S(2)}, u32[]{:S(2)}) %collective-permute-start.2) | collective-permute-done | bytes 24608 | tf_op jit(solution)/shard_map/ppermute | solution.py:16
  258.3 8.1 %reduce-scatter.15.cloned.1.call-done = bf16[96,64]{1,0:T(8,128)(2,1)} async-done(((bf16[192,64]{1,0:T(8,128)(2,1)}), bf16[96,64]{1,0:T(8,128)(2,1)}) %reduce-scatter.15.cloned.1.call-update) | async-done | bytes 12304
  267.2 5.2 %all-gather.2 = bf16[4,96,64]{1,2,0:T(8,128)(2,1)S(1)} all-gather(bf16[1,96,64]{1,2,0:T(8,128)(2,1)S(1)} %copy.154), channel_id=3, replica_groups=mesh['leaf'=4,'row'=2,'col'=4] {'col'}, dimensions={0}, use_global_device_ids=true | all-gather | bytes 61440 | tf_op jit(solution)/shard_map/all_gather | solution.py:193
  273.1 1.6 collective-permute-start.3
  274.6 2.4 collective-permute-done.3
  277.9 10.0 %reduce-scatter.17.cloned.1.call-done = bf16[96,64]{1,0:T(8,128)(2,1)} async-done(((bf16[192,64]{1,0:T(8,128)(2,1)}), bf16[96,64]{1,0:T(8,128)(2,1)}) %reduce-scatter.17.cloned.1.call-update) | async-done | bytes 12304
  289.3 3.3 %all-to-all-start.3 = ((f32[64,1,96]{2,1,0:T(1,128)}), f32[64,1,96]{2,1,0:T(1,128)S(1)}, u32[]{:S(2)}, u32[]{:S(2)}) async-start(f32[64,1,96]{2,1,0:T(1,128)} %bitcast.46), calls=%async_computation.4 | async-start | bytes 65536 | tf_op jit(solution)/shard_map/all_to_all | solution.py:197
  292.6 3.9 %all-to-all-done.3 = f32[64,1,96]{2,1,0:T(1,128)S(1)} async-done(((f32[64,1,96]{2,1,0:T(1,128)}), f32[64,1,96]{2,1,0:T(1,128)S(1)}, u32[]{:S(2)}, u32[]{:S(2)}) %all-to-all-start.3) | async-done | bytes 24608 | tf_op jit(solution)/shard_map/all_to_all | solution.py:197
  296.7 5.3 %all_gather.27 = bf16[16,4,192]{0,1,2:T(4,128)(2,1)S(1)} all-gather(bf16[16,4,96]{0,1,2:T(4,128)(2,1)S(1)} %bitcast.162), channel_id=1, replica_groups=mesh['leaf'=4,'row'=2,'col'=4] {'row'}, dimensions={2}, use_global_device_ids=true | all-gather | bytes 36864 | tf_op jit(solution)/shard_map/all_gather | solution.py:20
  302.0 1.5 collective-permute-start.4
  304.9 2.8 collective-permute-done.4
  (102 shorter events, 18.1 us)
Async XLA Ops:
  7.2 126.2 %copy-start = (bf16[4,96,768]{2,1,0:T(8,128)(2,1)S(1)}, bf16[4,96,768]{2,1,0:T(8,128)(2,1)}, u32[]{:S(2)}) copy-start(bf16[4,96,768]{2,1,0:T(8,128)(2,1)} %param.11) | copy-start | bytes 1769476
  7.2 13.4 %copy-start.5 = (s32[4,8]{1,0:T(4,128)S(1)}, s32[4,8]{1,0:T(4,128)}, u32[]{:S(2)}) copy-start(s32[4,8]{1,0:T(4,128)} %param.15) | copy-start | bytes 388
  18.4 21.0 %copy-start.2 = (bf16[4,96,384]{2,1,0:T(8,128)(2,1)S(1)}, bf16[4,96,384]{2,1,0:T(8,128)(2,1)}, u32[]{:S(2)}) copy-start(bf16[4,96,384]{2,1,0:T(8,128)(2,1)} %param.12) | copy-start | bytes 884740
  18.4 11.7 %collective-permute-start = (bf16[16,4,448]{0,1,2:T(4,128)(2,1)S(1)}, bf16[16,4,448]{0,1,2:T(4,128)(2,1)S(1)}, u32[]{:S(2)}, u32[]{:S(2)}) collective-permute-start(bf16[16,4,448]{0,1,2:T(4,128)(2,1)S(1)} %all_gather.21), channel_id=1, source_target_pairs={{0,8},{8,0},{16,24},{24,16},{1,9},{9,1},{17,25},{25,17},{2,10},{10... | collective-permute-start | bytes 172040 | tf_op jit(solution)/shard_map/ppermute | solution.py:16
  30.4 29.5 %copy-start.1 = (bf16[4,128,384]{2,1,0:T(8,128)(2,1)S(1)}, bf16[4,128,384]{2,1,0:T(8,128)(2,1)}, u32[]{:S(2)}) copy-start(bf16[4,128,384]{2,1,0:T(8,128)(2,1)} %param.13) | copy-start | bytes 1179652
  30.9 30.0 %copy-start.3 = (bf16[16,4,96]{2,1,0:T(4,128)(2,1)S(1)}, bf16[16,4,96]{2,1,0:T(4,128)(2,1)}, u32[]{:S(2)}) copy-start(bf16[16,4,96]{2,1,0:T(4,128)(2,1)} %param.8) | copy-start | bytes 36868
  32.2 7.3 %all-to-all-start = ((bf16[16,4,384]{2,0,1:T(8,128)(2,1)}), bf16[16,4,384]{2,0,1:T(8,128)(2,1)S(1)}, u32[]{:S(2)}, u32[]{:S(2)}) async-start(bf16[16,4,384]{2,0,1:T(8,128)(2,1)} %bitcast.141), calls=%async_computation | async-start | bytes 98304 | tf_op jit(solution)/shard_map/all_to_all | solution.py:114
  35.4 46.4 %reduce-scatter.11.cloned.1.call-start = ((), (), s32[]{:S(2)}) async-start(), calls=%async_computation.8 | async-start | bytes 163840 | tf_op jit(solution)/shard_map/reduce_scatter | solution.py:126
  55.9 4.0 %collective-permute-start.1 = (bf16[64,1,192]{2,0,1:T(8,128)(2,1)S(1)}, bf16[64,1,192]{2,0,1:T(8,128)(2,1)S(1)}, u32[]{:S(2)}, u32[]{:S(2)}) collective-permute-start(bf16[64,1,192]{2,0,1:T(8,128)(2,1)S(1)} %copy.141), channel_id=1, source_target_pairs={{0,8},{8,0},{16,24},{24,16},{1,9},{9,1},{17,25},{25,17},{2,10},{10... | collective-permute-start | bytes 73736 | tf_op jit(solution)/shard_map/ppermute | solution.py:16
  60.8 145.3 %reduce-scatter.13.cloned.1.call-start = ((), (), s32[]{:S(2)}) async-start(), calls=%async_computation.9 | async-start | bytes 442368
  124.5 1.1 copy-start.4
  207.6 7.2 %all-to-all-start.2 = ((f32[64,1,96]{2,1,0:T(1,128)}), f32[64,1,96]{2,1,0:T(1,128)S(1)}, u32[]{:S(2)}, u32[]{:S(2)}) async-start(f32[64,1,96]{2,1,0:T(1,128)} %bitcast.28), calls=%async_computation.3 | async-start | bytes 65536 | tf_op jit(solution)/shard_map/all_to_all | solution.py:163
  210.9 55.5 %reduce-scatter.15.cloned.1.call-start = ((), (), s32[]{:S(2)}) async-start(), calls=%async_computation.10 | async-start | bytes 73728
  253.4 4.0 %collective-permute-start.2 = (bf16[64,192]{1,0:T(8,128)(2,1)S(1)}, bf16[64,192]{1,0:T(8,128)(2,1)S(1)}, u32[]{:S(2)}, u32[]{:S(2)}) collective-permute-start(bf16[64,192]{1,0:T(8,128)(2,1)S(1)} %select_convert_fusion.1), channel_id=1, source_target_pairs={{0,8},{8,0},{16,24},{24,16},{1,9},{9,1},{17,25},{25,17},{2,10},{10... | collective-permute-start | bytes 73736 | tf_op jit(solution)/shard_map/ppermute | solution.py:16
  258.2 29.7 %reduce-scatter.17.cloned.1.call-start = ((), (), s32[]{:S(2)}) async-start(), calls=%async_computation.11 | async-start | bytes 73728
  273.1 4.0 %collective-permute-start.3 = (bf16[64,192]{1,0:T(8,128)(2,1)S(1)}, bf16[64,192]{1,0:T(8,128)(2,1)S(1)}, u32[]{:S(2)}, u32[]{:S(2)}) collective-permute-start(bf16[64,192]{1,0:T(8,128)(2,1)S(1)} %select_convert_fusion), channel_id=1, source_target_pairs={{0,8},{8,0},{16,24},{24,16},{1,9},{9,1},{17,25},{25,17},{2,10},{10... | collective-permute-start | bytes 73736 | tf_op jit(solution)/shard_map/ppermute | solution.py:16
  289.3 7.2 %all-to-all-start.3 = ((f32[64,1,96]{2,1,0:T(1,128)}), f32[64,1,96]{2,1,0:T(1,128)S(1)}, u32[]{:S(2)}, u32[]{:S(2)}) async-start(f32[64,1,96]{2,1,0:T(1,128)} %bitcast.46), calls=%async_computation.4 | async-start | bytes 65536 | tf_op jit(solution)/shard_map/all_to_all | solution.py:197
  302.0 5.7 %collective-permute-start.4 = (bf16[16,4,192]{0,1,2:T(4,128)(2,1)S(1)}, bf16[16,4,192]{0,1,2:T(4,128)(2,1)S(1)}, u32[]{:S(2)}, u32[]{:S(2)}) collective-permute-start(bf16[16,4,192]{0,1,2:T(4,128)(2,1)S(1)} %all_gather.27), channel_id=1, source_target_pairs={{0,8},{8,0},{16,24},{24,16},{1,9},{9,1},{17,25},{25,17},{2,10},{10... | collective-permute-start | bytes 73736 | tf_op jit(solution)/shard_map/ppermute | solution.py:16
Sparse Core Ops, SparseCore 0:
  60.9 20.8 reduce-scatter.10
  146.1 59.9 reduce-scatter.12
  258.3 8.0 reduce-scatter.14
  278.0 9.8 reduce-scatter.16
where the time goes:
time: 316 us; the launch traced here: 315 us
  blocking collectives  132 us (42%)
  waiting for transfers between devices  132 us (42%)
  starting transfers between devices  16.5 us (5%)
  local copies, waits for them, and re-layouts  15.4 us (5%)
  between operations  14.4 us (5%)
    unnamed x7, waiting for transfers between devices  78.3 us
    all_gather x1, blocking collectives, local(): lax.all_gather(joined_root, ('leaf', 'row'), axis=2, tiled=True)  41.1 us
    all_gather x1, blocking collectives, local(): lax.all_gather(solution_root.astype(jnp.bfloat16), ('leaf', 'row'), axis=...  32 us
    ppermute x5, waiting for transfers between devices, partner_2(): return lax.ppermute(block, axis, route)  21.1 us
    reduce_scatter x1, waiting for transfers between devices, local(): lax.psum_scatter(contract(forward_tile, off_matrix, 1, 1), 'col', scatter...  20.5 us
    all_gather x3, blocking collectives, group_gather(): merged = lax.all_gather(piece, 'row', axis=2, tiled=True)  19.3 us
    psum x1, blocking collectives, local(): lax.psum(contract(root_tile, root_matrix, 1, 1), 'col').astype(jnp.bfloat16)  11.2 us
    psum x1, blocking collectives, local(): lax.psum(contract(child_tile, child_matrix, 1, 1), 'col')  11.1 us
  transfers between devices with their start and end apart: 12, of which 12 were waited for; matrix products, arithmetic and copies ran while one was open for 1% of the time, Pallas kernels for 0%

commit v1 on v0

--- a/solution.py
+++ b/solution.py
@@ -1,6 +1,10 @@
+import functools
+
 import jax
 import jax.numpy as jnp
 from jax import lax
+from jax.experimental import pallas as pl
+from jax.experimental.pallas import tpu as pltpu
 from jax.sharding import PartitionSpec as P
 
 BLOCK_ROWS = 128
@@ -217,6 +221,375 @@
     return (solution_root, solution_child, leaf_solution)
 
 
+F32 = jnp.float32
+BF16 = jnp.bfloat16
+
+
+def inverse_table(block_map, blocks_total, places):
+    hit = block_map[..., None] == jnp.arange(blocks_total, dtype=jnp.int32)
+    return jnp.sum(jnp.where(hit, places[:, None] + 1, 0), axis=-2, dtype=jnp.int32) - 1
+
+
+def add_up(terms):
+    total = terms[0]
+    for term in terms[1:]:
+        total = total + term
+    return total
+
+
+def solve_kernel(
+    dims,
+    sub_table, root_table, leaf_table, child_map,
+    sub_in, rc_in, rr_in, root_hbm, child_hbm, off_hbm,
+    root_out, child_out, leaf_out,
+    root_w, child_w, off_w,
+    sub_buf, rc_buf, rr_buf,
+    p2_send, p2_recv, p3_send, p3_recv, pass_send, pass_buf,
+    tile_send, tile_recv, p4_send, p4_recv, p5_send, p5_recv,
+    sr_send, sr_recv, kn_send, kn_recv, p7_send, p7_recv, p8_send, p8_recv,
+    blocks, pieces,
+    load_sems, send_sems, recv_sems,
+):
+    n_leaf, n_row, n_col = dims
+    panel = sub_in.shape[1]
+    sep = rc_in.shape[2]
+    ranks = n_row * (n_leaf // 2)
+    rows_all = n_leaf * n_row
+    group = ranks * n_col
+    everyone = rows_all * n_col
+    right = panel * n_col
+    child_tile_blocks = child_w.shape[2] // BLOCK_ROWS
+    root_tile_blocks = root_w.shape[2] // BLOCK_ROWS
+    sep_blocks = child_tile_blocks * n_col
+    c = lax.axis_index("col")
+    leaf = lax.axis_index("leaf")
+    row = lax.axis_index("row")
+    half = n_leaf // 2
+    front = lax.div(leaf, half)
+    rank = lax.rem(leaf, half) * n_row + row
+    r = leaf * n_row + row
+    gid = c * ranks + rank
+    me = r * n_col + c
+
+    loads = [
+        pltpu.make_async_copy(child_hbm, child_w, load_sems.at[0]),
+        pltpu.make_async_copy(off_hbm, off_w, load_sems.at[1]),
+        pltpu.make_async_copy(root_hbm, root_w, load_sems.at[2]),
+    ]
+    for load in loads:
+        load.start()
+
+    def at_row(r2, c2):
+        return {"leaf": lax.div(r2, n_row), "row": lax.rem(r2, n_row), "col": c2}
+
+    def at_group(g2):
+        return at_row(front * ranks + lax.rem(g2, ranks), lax.div(g2, ranks))
+
+    def each(count, own, body):
+        def step(k, carry):
+            body(lax.rem(own + k, count))
+            return carry
+
+        lax.fori_loop(1, count, step, 0)
+
+    def push(source, target, phase, device):
+        pltpu.make_async_remote_copy(
+            src_ref=source,
+            dst_ref=target,
+            send_sem=send_sems.at[phase],
+            recv_sem=recv_sems.at[phase],
+            device_id=device,
+            device_id_type=pl.DeviceIdType.MESH,
+        ).start()
+
+    def drain(view, sem):
+        pltpu.make_async_copy(view, view, sem).wait()
+
+    barrier = pltpu.get_barrier_semaphore()
+
+    def greet(d):
+        pl.semaphore_signal(
+            barrier, inc=1, device_id=at_row(lax.div(d, n_col), lax.rem(d, n_col)),
+            device_id_type=pl.DeviceIdType.MESH,
+        )
+
+    each(everyone, me, greet)
+    pl.semaphore_wait(barrier, everyone - 1)
+
+    each(group, gid, lambda g2: push(rc_in.at[lax.div(g2, ranks)], rc_buf.at[gid], 1, at_group(g2)))
+    each(group, gid, lambda g2: push(sub_in, sub_buf.at[pl.ds(gid * n_col, n_col)], 0, at_group(g2)))
+    each(rows_all, r, lambda r2: push(rr_in, rr_buf.at[r], 2, at_row(r2, c)))
+    sub_buf[pl.ds(gid * n_col, n_col)] = sub_in[...]
+    rc_buf[gid] = rc_in[c]
+    rr_buf[r] = rr_in[...]
+    loads[0].wait()
+    drain(rc_buf.at[pl.ds(0, group - 1)], recv_sems.at[1])
+    drain(sub_buf.at[pl.ds(0, (group - 1) * n_col)], recv_sems.at[0])
+
+    def placed(p, block):
+        total = None
+        for h in range(2):
+            place = sub_table[2 * front + h, block]
+            value = sub_buf[p * ranks * n_col + jnp.maximum(place, 0)].astype(F32)
+            value = jnp.where(place >= 0, value, jnp.zeros_like(value))
+            total = value if total is None else total + value
+        return total
+
+    def rows_of(values):
+        return jnp.concatenate(values, 0)
+
+    x = jnp.concatenate(
+        [rows_of([rc_buf[p * ranks + k] for p in range(n_col)]).astype(F32) for k in range(ranks)], 1
+    )
+    x = x + jnp.concatenate(
+        [
+            rows_of([placed(p, c * child_tile_blocks + b) for p in range(n_col)])
+            for b in range(child_tile_blocks)
+        ],
+        1,
+    )
+    x = x.astype(BF16)
+    for q in range(n_col):
+        p2_send[q] = contract(x, child_w[q], 1, 1).astype(BF16)
+
+    each(group, gid, lambda g2: push(p2_send.at[lax.div(g2, ranks)], p2_recv.at[gid], 3, at_group(g2)))
+    p2_recv[gid] = p2_send[c]
+    tail = [placed(c, sep_blocks + q * ranks + rank) for q in range(n_col)]
+    loads[1].wait()
+    drain(p2_recv.at[pl.ds(0, group - 1)], recv_sems.at[3])
+    forward = [
+        add_up([p2_recv[c2 * ranks + k].astype(F32) for c2 in range(n_col)]).astype(BF16)
+        for k in range(ranks)
+    ]
+    y = jnp.concatenate([piece.astype(F32) for piece in forward], 1).astype(BF16)
+    for q in range(n_col):
+        z = contract(y, off_w[q], 1, 1).astype(BF16)
+        for p in range(n_col):
+            p3_send[p, q] = z[p * panel : (p + 1) * panel]
+
+    each(n_col, c, lambda c2: push(p3_send.at[c2], p3_recv.at[c], 4, at_row(r, c2)))
+    p3_recv[c] = p3_send[c]
+    drain(p3_recv.at[pl.ds(0, n_col - 1)], recv_sems.at[4])
+    for q in range(n_col):
+        total = add_up([p3_recv[c2, q].astype(F32) for c2 in range(n_col)])
+        pass_send[q] = (tail[q] - total).astype(BF16)
+
+    each(rows_all, r, lambda r2: push(pass_send, pass_buf.at[pl.ds(r * n_col, n_col)], 5, at_row(r2, c)))
+    pass_buf[pl.ds(r * n_col, n_col)] = pass_send[...]
+    drain(rr_buf.at[pl.ds(0, rows_all - 1)], recv_sems.at[2])
+    x = jnp.concatenate(
+        [rr_buf[k].reshape(right, sep).astype(F32) for k in range(rows_all)], 1
+    )
+    drain(pass_buf.at[pl.ds(0, (rows_all - 1) * n_col)], recv_sems.at[5])
+
+    def passed(block):
+        total = None
+        for f in range(2):
+            place = root_table[f, block]
+            value = pass_buf[jnp.maximum(place, 0)].astype(F32)
+            value = jnp.where(place >= 0, value, jnp.zeros_like(value))
+            total = value if total is None else total + value
+        return total
+
+    x = x + jnp.concatenate(
+        [
+            rows_of([passed(q * root_tile_blocks + b) for q in range(n_col)])
+            for b in range(root_tile_blocks)
+        ],
+        1,
+    )
+    tile_send[...] = x.astype(BF16).reshape(tile_send.shape)
+
+    each(n_col, c, lambda c2: push(tile_send.at[c2], tile_recv.at[c], 6, at_row(r, c2)))
+    tile_recv[c] = tile_send[c]
+    loads[2].wait()
+    drain(tile_recv.at[pl.ds(0, n_col - 1)], recv_sems.at[6])
+    x = tile_recv[...].reshape(right, root_w.shape[2])
+    for q in range(n_col):
+        p4_send[q] = contract(x, root_w[q], 1, 1).astype(BF16)
+
+    each(n_col, c, lambda c2: push(p4_send, p4_recv.at[c], 7, at_row(r, c2)))
+    p4_recv[c] = p4_send[...]
+    drain(p4_recv.at[pl.ds(0, n_col - 1)], recv_sems.at[7])
+    total = None
+    for q in range(n_col):
+        piece = add_up([p4_recv[c2, q].astype(F32) for c2 in range(n_col)]).astype(BF16)
+        term = contract(piece, root_w[q], 1, 0)
+        total = term if total is None else total + term
+    for r2 in range(rows_all):
+        piece = total[:, r2 * sep : (r2 + 1) * sep].astype(BF16)
+        for p in range(n_col):
+            p5_send[r2 * n_col + p] = piece[p * panel : (p + 1) * panel]
+
+    each(
+        everyone, me,
+        lambda d: push(
+            p5_send.at[d], p5_recv.at[c * rows_all + r], 8,
+            at_row(lax.div(d, n_col), lax.rem(d, n_col)),
+        ),
+    )
+    p5_recv[c * rows_all + r] = p5_send[me]
+    drain(p5_recv.at[pl.ds(0, everyone - 1)], recv_sems.at[8])
+    for q in range(n_col):
+        total = add_up([p5_recv[q * rows_all + k].astype(F32) for k in range(rows_all)])
+        root_out[q] = total
+        sr_send[q] = total.astype(BF16)
+
+    each(rows_all, r, lambda r2: push(sr_send, sr_recv.at[r], 9, at_row(r2, c)))
+    sr_recv[r] = sr_send[...]
+    drain(sr_recv.at[pl.ds(0, rows_all - 1)], recv_sems.at[9])
+    x = jnp.concatenate(
+        [sr_recv[k].reshape(right, sep).astype(F32) for k in range(rows_all)], 1
+    ).astype(BF16)
+    for q in range(n_col):
+        for b in range(root_tile_blocks):
+            blocks[sep_blocks + q * root_tile_blocks + b] = x[
+                q * panel : (q + 1) * panel, b * BLOCK_ROWS : (b + 1) * BLOCK_ROWS
+            ]
+    for q in range(n_col):
+        kn_send[q] = blocks[sep_blocks + child_map[front, q * ranks + rank]]
+
+    each(n_col, c, lambda c2: push(kn_send, kn_recv.at[c], 10, at_row(r, c2)))
+    kn_recv[c] = kn_send[...]
+    drain(kn_recv.at[pl.ds(0, n_col - 1)], recv_sems.at[10])
+    total = None
+    for q in range(n_col):
+        term = contract(rows_of([kn_recv[p, q] for p in range(n_col)]), off_w[q], 1, 0)
+        total = term if total is None else total + term
+    for k in range(ranks):
+        own = jnp.where(rank == k, forward[k].astype(F32), jnp.zeros(forward[k].shape, F32))
+        p7_send[k] = (own - total[:, k * sep : (k + 1) * sep]).astype(BF16)
+
+    each(group, gid, lambda g2: push(p7_send.at[lax.rem(g2, ranks)], p7_recv.at[gid], 11, at_group(g2)))
+    p7_recv[gid] = p7_send[rank]
+    drain(p7_recv.at[pl.ds(0, group - 1)], recv_sems.at[11])
+    total = None
+    for q in range(n_col):
+        piece = add_up([p7_recv[q * ranks + k].astype(F32) for k in range(ranks)]).astype(BF16)
+        term = contract(piece, child_w[q], 1, 0)
+        total = term if total is None else total + term
+    p8_send[...] = total.astype(BF16).reshape(p8_send.shape)
+
+    each(group, gid, lambda g2: push(p8_send.at[lax.div(g2, ranks)], p8_recv.at[gid], 12, at_group(g2)))
+    p8_recv[gid] = p8_send[c]
+    drain(p8_recv.at[pl.ds(0, group - 1)], recv_sems.at[12])
+    for q in range(n_col):
+        total = add_up([p8_recv[q * ranks + k].astype(F32) for k in range(ranks)])
+        for k in range(ranks):
+            pieces[q, k] = total[:, k * sep : (k + 1) * sep]
+        child_out[q] = pieces[q, rank]
+        total = total.astype(BF16)
+        for b in range(child_tile_blocks):
+            blocks[q * child_tile_blocks + b] = total[:, b * BLOCK_ROWS : (b + 1) * BLOCK_ROWS]
+    for q in range(n_col):
+        leaf_out[q] = blocks[leaf_table[leaf, q * n_row + row]]
+
+    drain(rc_buf.at[pl.ds(0, group - 1)], send_sems.at[1])
+    drain(sub_buf.at[pl.ds(0, (group - 1) * n_col)], send_sems.at[0])
+    drain(rr_buf.at[pl.ds(0, rows_all - 1)], send_sems.at[2])
+    drain(p2_recv.at[pl.ds(0, group - 1)], send_sems.at[3])
+    drain(p3_recv.at[pl.ds(0, n_col - 1)], send_sems.at[4])
+    drain(pass_buf.at[pl.ds(0, (rows_all - 1) * n_col)], send_sems.at[5])
+    drain(tile_recv.at[pl.ds(0, n_col - 1)], send_sems.at[6])
+    drain(p4_recv.at[pl.ds(0, n_col - 1)], send_sems.at[7])
+    drain(p5_recv.at[pl.ds(0, everyone - 1)], send_sems.at[8])
+    drain(sr_recv.at[pl.ds(0, rows_all - 1)], send_sems.at[9])
+    drain(kn_recv.at[pl.ds(0, n_col - 1)], send_sems.at[10])
+    drain(p7_recv.at[pl.ds(0, group - 1)], send_sems.at[11])
+    drain(p8_recv.at[pl.ds(0, group - 1)], send_sems.at[12])
+
+
+def fused(
+    rhs_root, rhs_child, subtree_update, inv_root, inv_child, off_child, child_map, subtree_map
+):
+    n_col = lax.axis_size("col")
+    n_row = lax.axis_size("row")
+    n_leaf = lax.axis_size("leaf")
+    panel = rhs_child.shape[0]
+    right = panel * n_col
+    sep = rhs_child.shape[2]
+    ranks = n_row * (n_leaf // 2)
+    rows_all = n_leaf * n_row
+    group = ranks * n_col
+    everyone = rows_all * n_col
+    root_width = inv_root.shape[2]
+    child_width = inv_child.shape[2]
+    sep_blocks = child_width * n_col // BLOCK_ROWS
+    root_blocks = root_width * n_col // BLOCK_ROWS
+    sub_count = subtree_map.shape[1]
+    upd_count = child_map.shape[1]
+
+    number = jnp.arange(sub_count, dtype=jnp.int32)
+    half = (jnp.arange(4, dtype=jnp.int32) % 2)[:, None]
+    within = (number % n_row) * n_col + number // n_row
+    sub_table = inverse_table(subtree_map, sep_blocks + upd_count, within)
+    sub_table = jnp.where(sub_table >= 0, sub_table + half * n_row * n_col, -1)
+    number = jnp.arange(upd_count, dtype=jnp.int32)
+    root_table = inverse_table(child_map, root_blocks, (number % ranks) * n_col + number // ranks)
+    child = jnp.arange(2, dtype=jnp.int32)[:, None]
+    root_table = jnp.where(root_table >= 0, root_table + child * ranks * n_col, -1)
+    beyond = jnp.clip(subtree_map - sep_blocks, 0)
+    known = jnp.take_along_axis(jnp.repeat(child_map, 2, axis=0), beyond, axis=1)
+    leaf_table = jnp.where(subtree_map < sep_blocks, subtree_map, sep_blocks + known)
+
+    def turn(array):
+        return array.transpose(1, 0, 2)
+
+    smem = pl.BlockSpec(memory_space=pltpu.SMEM)
+    vmem = pl.BlockSpec(memory_space=pltpu.VMEM)
+    hbm = pl.BlockSpec(memory_space=pl.ANY)
+    buffer = lambda *shape: pltpu.VMEM(shape, BF16)
+    outs = pl.pallas_call(
+        functools.partial(solve_kernel, (n_leaf, n_row, n_col)),
+        out_shape=(
+            jax.ShapeDtypeStruct((n_col, panel, sep), F32),
+            jax.ShapeDtypeStruct((n_col, panel, sep), F32),
+            jax.ShapeDtypeStruct((n_col, panel, BLOCK_ROWS), BF16),
+        ),
+        in_specs=[smem] * 4 + [vmem] * 3 + [hbm] * 3,
+        out_specs=(vmem, vmem, vmem),
+        scratch_shapes=[
+            buffer(*inv_root.shape), buffer(*inv_child.shape), buffer(*off_child.shape),
+            buffer(group * n_col, panel, BLOCK_ROWS),
+            buffer(group, panel, sep),
+            buffer(rows_all, n_col, panel, sep),
+            buffer(n_col, right, sep), buffer(group, right, sep),
+            buffer(n_col, n_col, panel, BLOCK_ROWS), buffer(n_col, n_col, panel, BLOCK_ROWS),
+            buffer(n_col, panel, BLOCK_ROWS), buffer(rows_all * n_col, panel, BLOCK_ROWS),
+            buffer(n_col, panel, root_width), buffer(n_col, panel, root_width),
+            buffer(n_col, right, sep), buffer(n_col, n_col, right, sep),
+            buffer(everyone, panel, sep), buffer(everyone, panel, sep),
+            buffer(n_col, panel, sep), buffer(rows_all, n_col, panel, sep),
+            buffer(n_col, panel, BLOCK_ROWS), buffer(n_col, n_col, panel, BLOCK_ROWS),
+            buffer(ranks, right, sep), buffer(group, right, sep),
+            buffer(n_col, panel, child_width), buffer(group, panel, child_width),
+            buffer(sep_blocks + root_blocks, panel, BLOCK_ROWS),
+            pltpu.VMEM((n_col, ranks, panel, sep), F32),
+            pltpu.SemaphoreType.DMA((3,)),
+            pltpu.SemaphoreType.DMA((13,)),
+            pltpu.SemaphoreType.DMA((13,)),
+        ],
+        compiler_params=pltpu.CompilerParams(
+            collective_id=0, has_side_effects=True, vmem_limit_bytes=32 * 1024 * 1024
+        ),
+    )(
+        sub_table, root_table, leaf_table, child_map,
+        turn(subtree_update), turn(rhs_child), turn(rhs_root), inv_root, inv_child, off_child,
+    )
+    return tuple(turn(out) for out in outs)
+
+
+def body(*arrays):
+    whole_blocks = (
+        lax.axis_size("leaf") == 4
+        and arrays[2].shape[2] == BLOCK_ROWS
+        and arrays[4].shape[2] % BLOCK_ROWS == 0
+        and arrays[0].shape[0] % 16 == 0
+        and arrays[0].shape[2] % 16 == 0
+    )
+    return (fused if whole_blocks else local)(*arrays)
+
+
 def solution(mesh):
     in_specs = (
         P("col", None, ("leaf", "row")),
@@ -233,4 +606,4 @@
         P("col", None, ("leaf", "row")),
         P("col", None, ("leaf", "row")),
     )
-    return jax.shard_map(local, mesh=mesh, in_specs=in_specs, out_specs=out_specs, check_vma=False)
+    return jax.shard_map(body, mesh=mesh, in_specs=in_specs, out_specs=out_specs, check_vma=False)

time: 316 us -> 66.3 us (0.21)
  blocking collectives: 132 us -> 0 us
  waiting for transfers between devices: 132 us -> 0 us
  Pallas kernels: 0 us -> 60.3 us
  starting transfers between devices: 16.5 us -> 0 us
  between operations: 14.4 us -> 0.73 us
  local copies, waits for them, and re-layouts: 15.4 us -> 4.71 us
    all_gather x7 -> x0, blocking collectives: 103 us -> none  [the longest x1 41.1 us: local(): lax.all_gather(joined_root, ('leaf', 'row'), axis=2, tiled=True)]
    unnamed x7 -> x0, waiting for transfers between devices: 78.3 us -> none
    pallas_call x0 -> x1, Pallas kernels: none -> 60.3 us  [fused(): pl.pallas_call(functools.partial(solve_kernel, (n_leaf, n_row, n_col)), o...]
    psum x2 -> x0, blocking collectives: 22.3 us -> none  [the longest x1 11.2 us: local(): lax.psum(contract(root_tile, root_matrix, 1, 1), 'col').astype(jnp.bfloat16)]
    ppermute x5 -> x0, waiting for transfers between devices: 21.1 us -> none  [partner_2(): return lax.ppermute(block, axis, route)]
    reduce_scatter x1 -> x0, waiting for transfers between devices: 20.5 us -> none  [local(): lax.psum_scatter(contract(forward_tile, off_matrix, 1, 1), 'col', scatter...]
    all_to_all x3 -> x0, waiting for transfers between devices: 11.7 us -> none  [the longest x1 3.95 us: local(): lax.all_to_all(child_sep.reshape(panel_width, n_col, child_width), 'col',...]
    all_to_all x3 -> x0, starting transfers between devices: 9.8 us -> none  [the longest x1 3.27 us: local(): lax.all_to_all(child_sep.reshape(panel_width, n_col, child_width), 'col',...]
  transfers between devices with their start and end apart: 12 -> 0, of which waited for: 12 -> 0; matrix products, arithmetic and copies ran while one was open for 1% -> 0% of each run, Pallas kernels for 0% -> 0%
where the time goes in v1:
time: 66.3 us; the launch traced here: 66.1 us
  Pallas kernels  60.3 us (91%)
  local copies, waits for them, and re-layouts  4.71 us (7%)
  between operations  0.73 us (1%)
    pallas_call x1, Pallas kernels, fused(): pl.pallas_call(functools.partial(solve_kernel, (n_leaf, n_row, n_col)), o...  60.3 us
    unnamed x20, local copies, waits for them, and re-layouts  3.78 us

profile of v1, /device:TPU:0, one launch (start us, length us, event | category | flops | bytes accessed | tf_op | source)
XLA Modules:
  0.0 66.1 jit_solution(11841606302327547891)
XLA Ops:
  0.7 0.0 copy-start.3
  0.7 0.7 copy-done.3
  1.3 0.0 copy-start.4
  1.3 0.1 select_reduce_fusion
  1.4 0.1 compare_select_fusion.1.root_table
  1.5 0.5 copy-done.4
  2.0 0.1 select_reduce_fusion.1
  2.1 0.1 add_select_fusion.sub_table
  2.2 0.1 reshape.44
  2.3 0.0 copy-start.5
  2.3 0.0 copy-start
  2.3 0.0 copy-start.1
  2.3 0.0 copy-start.2
  2.3 0.8 %gather_fusion = s32[32]{0:T(128)S(1)} fusion(s32[4,16]{1,0:T(4,128)S(1)} %bitcast.19, s32[32]{0:T(128)S(1)} %reshape.44), kind=kCustom, calls=%fused_computation | custom fusion | bytes 512 | tf_op jit(solution)/shard_map/jit(take_along_axis)/gather | solution.py:532
  3.1 0.1 reshape.47
  3.2 0.0 copy-done.5
  3.2 0.0 copy-start.6
  3.2 0.0 copy-start.7
  3.2 0.7 %copy-done.6 = bf16[16,4,96]{2,1,0:T(4,128)(2,1)S(1)} copy-done((bf16[16,4,96]{2,1,0:T(4,128)(2,1)S(1)}, bf16[16,4,96]{2,1,0:T(4,128)(2,1)}, u32[]{:S(2)}) %copy-start.6) | copy-done | bytes 12312
  3.9 0.0 copy-done.7
  3.9 0.0 copy-done
  3.9 0.0 copy-done.1
  3.9 0.0 copy-done.2
  3.9 60.3 %shard_map.103 = (f32[4,16,96]{2,1,0:T(8,128)S(1)}, f32[4,16,96]{2,1,0:T(8,128)S(1)}, bf16[4,16,128]{2,1,0:T(8,128)(2,1)S(1)}) custom-call(s32[4,28]{1,0:T(4,128)S(1)} %add_select_fusion.sub_table, s32[2,24]{1,0:T(2,128)S(1)} %compare_select_fusion.1.root_table, s32[4,8]{1,0:T(4,128)S(1)} %compare_select_fusion.leaf_table, s32[2,16]{1,0:T(2,128)S(1)} %copy-done.3, ...), custom_call_target="tpu_custom_call" | custom-call | tf_op jit(solution)/shard_map/pallas_call | solution.py:542
  64.2 0.6 copy.26
  64.9 0.6 copy.27
  65.5 0.6 copy.28
  (9 shorter events, 0.1 us)
Async XLA Ops:
  0.7 0.7 %copy-start.3 = (s32[2,16]{1,0:T(2,128)S(1)}, s32[2,16]{1,0:T(2,128)}, u32[]{:S(2)}) copy-start(s32[2,16]{1,0:T(2,128)} %child_map.1) | copy-start | bytes 388
  1.3 0.7 %copy-start.4 = (s32[4,8]{1,0:T(4,128)S(1)}, s32[4,8]{1,0:T(4,128)}, u32[]{:S(2)}) copy-start(s32[4,8]{1,0:T(4,128)} %param.15) | copy-start | bytes 388
  2.3 0.9 %copy-start.5 = (bf16[16,4,128]{2,1,0:T(4,128)(2,1)S(1)}, bf16[16,4,128]{2,1,0:T(4,128)(2,1)}, u32[]{:S(2)}) copy-start(bf16[16,4,128]{2,1,0:T(4,128)(2,1)} %param.10) | copy-start | bytes 49156
  2.3 1.6 %copy-start = (bf16[4,96,768]{2,1,0:T(8,128)(2,1)S(1)}, bf16[4,96,768]{2,1,0:T(8,128)(2,1)}, u32[]{:S(2)}) copy-start(bf16[4,96,768]{2,1,0:T(8,128)(2,1)} %root_hbm.1) | copy-start | bytes 1769476
  2.3 1.6 %copy-start.1 = (bf16[4,128,384]{2,1,0:T(8,128)(2,1)S(1)}, bf16[4,128,384]{2,1,0:T(8,128)(2,1)}, u32[]{:S(2)}) copy-start(bf16[4,128,384]{2,1,0:T(8,128)(2,1)} %off_hbm.1) | copy-start | bytes 1179652
  2.3 1.6 %copy-start.2 = (bf16[4,96,384]{2,1,0:T(8,128)(2,1)S(1)}, bf16[4,96,384]{2,1,0:T(8,128)(2,1)}, u32[]{:S(2)}) copy-start(bf16[4,96,384]{2,1,0:T(8,128)(2,1)} %child_hbm.1) | copy-start | bytes 884740
  3.2 0.7 %copy-start.6 = (bf16[16,4,96]{2,1,0:T(4,128)(2,1)S(1)}, bf16[16,4,96]{2,1,0:T(4,128)(2,1)}, u32[]{:S(2)}) copy-start(bf16[16,4,96]{2,1,0:T(4,128)(2,1)} %param.8) | copy-start | bytes 36868
  3.2 0.7 %copy-start.7 = (bf16[16,4,96]{2,1,0:T(4,128)(2,1)S(1)}, bf16[16,4,96]{2,1,0:T(4,128)(2,1)}, u32[]{:S(2)}) copy-start(bf16[16,4,96]{2,1,0:T(4,128)(2,1)} %param.9) | copy-start | bytes 36868

commit v2 on v1

--- a/solution.py
+++ b/solution.py
@@ -245,10 +245,10 @@
     root_w, child_w, off_w,
     sub_buf, rc_buf, rr_buf,
     p2_send, p2_recv, p3_send, p3_recv, pass_send, pass_buf,
-    tile_send, tile_recv, p4_send, p4_recv, p5_send, p5_recv,
-    sr_send, sr_recv, kn_send, kn_recv, p7_send, p7_recv, p8_send, p8_recv,
+    fw_send, fw_recv, p5_send, p5_recv,
+    sr_send, sr_recv, p7_send, p7_recv, p8_send, p8_recv,
     blocks, pieces,
-    load_sems, send_sems, recv_sems,
+    load_sems, send_sems, recv_sems, share_sems, shared_sems,
 ):
     n_leaf, n_row, n_col = dims
     panel = sub_in.shape[1]
@@ -256,10 +256,9 @@
     ranks = n_row * (n_leaf // 2)
     rows_all = n_leaf * n_row
     group = ranks * n_col
-    everyone = rows_all * n_col
     right = panel * n_col
-    child_tile_blocks = child_w.shape[2] // BLOCK_ROWS
-    root_tile_blocks = root_w.shape[2] // BLOCK_ROWS
+    child_tile_blocks = child_w.shape[3] // BLOCK_ROWS
+    root_tile_blocks = root_w.shape[3] // BLOCK_ROWS
     sep_blocks = child_tile_blocks * n_col
     c = lax.axis_index("col")
     leaf = lax.axis_index("leaf")
@@ -269,12 +268,11 @@
     rank = lax.rem(leaf, half) * n_row + row
     r = leaf * n_row + row
     gid = c * ranks + rank
-    me = r * n_col + c
 
     loads = [
-        pltpu.make_async_copy(child_hbm, child_w, load_sems.at[0]),
-        pltpu.make_async_copy(off_hbm, off_w, load_sems.at[1]),
-        pltpu.make_async_copy(root_hbm, root_w, load_sems.at[2]),
+        pltpu.make_async_copy(child_hbm, child_w.at[c], load_sems.at[0]),
+        pltpu.make_async_copy(off_hbm, off_w.at[c], load_sems.at[1]),
+        pltpu.make_async_copy(root_hbm, root_w.at[c], load_sems.at[2]),
     ]
     for load in loads:
         load.start()
@@ -307,14 +305,43 @@
 
     barrier = pltpu.get_barrier_semaphore()
 
-    def greet(d):
+    def greet(device):
         pl.semaphore_signal(
-            barrier, inc=1, device_id=at_row(lax.div(d, n_col), lax.rem(d, n_col)),
+            barrier, inc=1, device_id=device, device_id_type=pl.DeviceIdType.MESH
+        )
+
+    pair = c + 1 - 2 * lax.rem(c, 2)
+    across = lax.rem(c + 2, n_col)
+
+    def hand(weights, slot, number, kind, c2):
+        pltpu.make_async_remote_copy(
+            src_ref=weights.at[slot],
+            dst_ref=weights.at[slot],
+            send_sem=share_sems.at[number, kind],
+            recv_sem=shared_sems.at[number, kind],
+            device_id=at_row(r, c2),
             device_id_type=pl.DeviceIdType.MESH,
-        )
-
-    each(everyone, me, greet)
-    pl.semaphore_wait(barrier, everyone - 1)
+        ).start()
+
+    def share(weights, number):
+        hand(weights, c, number, 0, across)
+        hand(weights, c, number, 1, pair)
+
+    def relay(weights, number):
+        drain(weights.at[across], shared_sems.at[number, 0])
+        hand(weights, across, number, 2, pair)
+
+    def settle(weights, number):
+        drain(weights.at[0], shared_sems.at[number, 1])
+        drain(weights.at[0], shared_sems.at[number, 2])
+
+    def flat(weights, c2):
+        return weights[c2].reshape(-1, weights.shape[3])
+
+    each(group, gid, lambda g2: greet(at_group(g2)))
+    for k in range(ranks):
+        greet(at_row((1 - front) * ranks + k, c))
+    pl.semaphore_wait(barrier, group - 1 + ranks)
 
     each(group, gid, lambda g2: push(rc_in.at[lax.div(g2, ranks)], rc_buf.at[gid], 1, at_group(g2)))
     each(group, gid, lambda g2: push(sub_in, sub_buf.at[pl.ds(gid * n_col, n_col)], 0, at_group(g2)))
@@ -322,6 +349,8 @@
     sub_buf[pl.ds(gid * n_col, n_col)] = sub_in[...]
     rc_buf[gid] = rc_in[c]
     rr_buf[r] = rr_in[...]
+    loads[2].wait()
+    share(root_w, 2)
     loads[0].wait()
     drain(rc_buf.at[pl.ds(0, group - 1)], recv_sems.at[1])
     drain(sub_buf.at[pl.ds(0, (group - 1) * n_col)], recv_sems.at[0])
@@ -350,7 +379,7 @@
     )
     x = x.astype(BF16)
     for q in range(n_col):
-        p2_send[q] = contract(x, child_w[q], 1, 1).astype(BF16)
+        p2_send[q] = contract(x, child_w[c, q], 1, 1).astype(BF16)
 
     each(group, gid, lambda g2: push(p2_send.at[lax.div(g2, ranks)], p2_recv.at[gid], 3, at_group(g2)))
     p2_recv[gid] = p2_send[c]
@@ -363,12 +392,17 @@
     ]
     y = jnp.concatenate([piece.astype(F32) for piece in forward], 1).astype(BF16)
     for q in range(n_col):
-        z = contract(y, off_w[q], 1, 1).astype(BF16)
+        z = contract(y, off_w[c, q], 1, 1).astype(BF16)
         for p in range(n_col):
             p3_send[p, q] = z[p * panel : (p + 1) * panel]
 
     each(n_col, c, lambda c2: push(p3_send.at[c2], p3_recv.at[c], 4, at_row(r, c2)))
     p3_recv[c] = p3_send[c]
+    own = add_up([p2_recv[c2 * ranks + rank].astype(F32) for c2 in range(n_col)])
+    fw_send[...] = own.astype(BF16).reshape(fw_send.shape)
+    each(n_col, c, lambda c2: push(fw_send.at[c2], fw_recv.at[c], 6, at_row(r, c2)))
+    fw_recv[c] = fw_send[c]
+    share(off_w, 1)
     drain(p3_recv.at[pl.ds(0, n_col - 1)], recv_sems.at[4])
     for q in range(n_col):
         total = add_up([p3_recv[c2, q].astype(F32) for c2 in range(n_col)])
@@ -376,6 +410,7 @@
 
     each(rows_all, r, lambda r2: push(pass_send, pass_buf.at[pl.ds(r * n_col, n_col)], 5, at_row(r2, c)))
     pass_buf[pl.ds(r * n_col, n_col)] = pass_send[...]
+    relay(root_w, 2)
     drain(rr_buf.at[pl.ds(0, rows_all - 1)], recv_sems.at[2])
     x = jnp.concatenate(
         [rr_buf[k].reshape(right, sep).astype(F32) for k in range(rows_all)], 1
@@ -398,46 +433,32 @@
         ],
         1,
     )
-    tile_send[...] = x.astype(BF16).reshape(tile_send.shape)
-
-    each(n_col, c, lambda c2: push(tile_send.at[c2], tile_recv.at[c], 6, at_row(r, c2)))
-    tile_recv[c] = tile_send[c]
-    loads[2].wait()
-    drain(tile_recv.at[pl.ds(0, n_col - 1)], recv_sems.at[6])
-    x = tile_recv[...].reshape(right, root_w.shape[2])
-    for q in range(n_col):
-        p4_send[q] = contract(x, root_w[q], 1, 1).astype(BF16)
-
-    each(n_col, c, lambda c2: push(p4_send, p4_recv.at[c], 7, at_row(r, c2)))
-    p4_recv[c] = p4_send[...]
-    drain(p4_recv.at[pl.ds(0, n_col - 1)], recv_sems.at[7])
-    total = None
-    for q in range(n_col):
-        piece = add_up([p4_recv[c2, q].astype(F32) for c2 in range(n_col)]).astype(BF16)
-        term = contract(piece, root_w[q], 1, 0)
-        total = term if total is None else total + term
-    for r2 in range(rows_all):
-        piece = total[:, r2 * sep : (r2 + 1) * sep].astype(BF16)
-        for p in range(n_col):
-            p5_send[r2 * n_col + p] = piece[p * panel : (p + 1) * panel]
-
-    each(
-        everyone, me,
-        lambda d: push(
-            p5_send.at[d], p5_recv.at[c * rows_all + r], 8,
-            at_row(lax.div(d, n_col), lax.rem(d, n_col)),
-        ),
-    )
-    p5_recv[c * rows_all + r] = p5_send[me]
-    drain(p5_recv.at[pl.ds(0, everyone - 1)], recv_sems.at[8])
-    for q in range(n_col):
-        total = add_up([p5_recv[q * rows_all + k].astype(F32) for k in range(rows_all)])
+    x = x.astype(BF16)
+    settle(root_w, 2)
+    root_forward = add_up(
+        [
+            contract(x[c2 * panel : (c2 + 1) * panel], flat(root_w, c2), 1, 1)
+            for c2 in range(n_col)
+        ]
+    ).astype(BF16)
+    for c2 in range(n_col):
+        total = contract(root_forward, flat(root_w, c2), 1, 0)
+        for r2 in range(rows_all):
+            p5_send[r2, c2] = total[:, r2 * sep : (r2 + 1) * sep].astype(BF16)
+
+    each(rows_all, r, lambda r2: push(p5_send.at[r2], p5_recv.at[r], 7, at_row(r2, c)))
+    p5_recv[r] = p5_send[r]
+    share(child_w, 0)
+    drain(p5_recv.at[pl.ds(0, rows_all - 1)], recv_sems.at[7])
+    for q in range(n_col):
+        total = add_up([p5_recv[k, q].astype(F32) for k in range(rows_all)])
         root_out[q] = total
         sr_send[q] = total.astype(BF16)
 
-    each(rows_all, r, lambda r2: push(sr_send, sr_recv.at[r], 9, at_row(r2, c)))
+    each(rows_all, r, lambda r2: push(sr_send, sr_recv.at[r], 8, at_row(r2, c)))
     sr_recv[r] = sr_send[...]
-    drain(sr_recv.at[pl.ds(0, rows_all - 1)], recv_sems.at[9])
+    relay(off_w, 1)
+    drain(sr_recv.at[pl.ds(0, rows_all - 1)], recv_sems.at[8])
     x = jnp.concatenate(
         [sr_recv[k].reshape(right, sep).astype(F32) for k in range(rows_all)], 1
     ).astype(BF16)
@@ -446,35 +467,37 @@
             blocks[sep_blocks + q * root_tile_blocks + b] = x[
                 q * panel : (q + 1) * panel, b * BLOCK_ROWS : (b + 1) * BLOCK_ROWS
             ]
-    for q in range(n_col):
-        kn_send[q] = blocks[sep_blocks + child_map[front, q * ranks + rank]]
-
-    each(n_col, c, lambda c2: push(kn_send, kn_recv.at[c], 10, at_row(r, c2)))
-    kn_recv[c] = kn_send[...]
-    drain(kn_recv.at[pl.ds(0, n_col - 1)], recv_sems.at[10])
-    total = None
-    for q in range(n_col):
-        term = contract(rows_of([kn_recv[p, q] for p in range(n_col)]), off_w[q], 1, 0)
-        total = term if total is None else total + term
-    for k in range(ranks):
-        own = jnp.where(rank == k, forward[k].astype(F32), jnp.zeros(forward[k].shape, F32))
-        p7_send[k] = (own - total[:, k * sep : (k + 1) * sep]).astype(BF16)
-
-    each(group, gid, lambda g2: push(p7_send.at[lax.rem(g2, ranks)], p7_recv.at[gid], 11, at_group(g2)))
-    p7_recv[gid] = p7_send[rank]
-    drain(p7_recv.at[pl.ds(0, group - 1)], recv_sems.at[11])
-    total = None
-    for q in range(n_col):
-        piece = add_up([p7_recv[q * ranks + k].astype(F32) for k in range(ranks)]).astype(BF16)
-        term = contract(piece, child_w[q], 1, 0)
-        total = term if total is None else total + term
-    p8_send[...] = total.astype(BF16).reshape(p8_send.shape)
-
-    each(group, gid, lambda g2: push(p8_send.at[lax.div(g2, ranks)], p8_recv.at[gid], 12, at_group(g2)))
-    p8_recv[gid] = p8_send[c]
-    drain(p8_recv.at[pl.ds(0, group - 1)], recv_sems.at[12])
-    for q in range(n_col):
-        total = add_up([p8_recv[q * ranks + k].astype(F32) for k in range(ranks)])
+    known = jnp.concatenate(
+        [blocks[sep_blocks + child_map[front, q * ranks + rank]] for q in range(n_col)], 1
+    )
+    settle(off_w, 1)
+    for c2 in range(n_col):
+        total = contract(known, flat(off_w, c2), 1, 0)
+        for k in range(ranks):
+            p7_send[k, c2] = total[:, k * sep : (k + 1) * sep].astype(BF16)
+
+    def each_rank(body):
+        each(ranks, rank, lambda k: body(k, at_row(front * ranks + k, c)))
+
+    each_rank(lambda k, device: push(p7_send.at[k], p7_recv.at[rank], 9, device))
+    p7_recv[rank] = p7_send[rank]
+    relay(child_w, 0)
+    drain(fw_recv.at[pl.ds(0, n_col - 1)], recv_sems.at[6])
+    drain(p7_recv.at[pl.ds(0, ranks - 1)], recv_sems.at[9])
+    back = []
+    for q in range(n_col):
+        total = add_up([p7_recv[k, q].astype(F32) for k in range(ranks)])
+        back.append(fw_recv[q].astype(F32) - total)
+    back = jnp.concatenate(back, 1).astype(BF16)
+    settle(child_w, 0)
+    for c2 in range(n_col):
+        p8_send[c2] = contract(back, flat(child_w, c2), 1, 0).astype(BF16)
+
+    each_rank(lambda k, device: push(p8_send, p8_recv.at[rank], 10, device))
+    p8_recv[rank] = p8_send[...]
+    drain(p8_recv.at[pl.ds(0, ranks - 1)], recv_sems.at[10])
+    for q in range(n_col):
+        total = add_up([p8_recv[k, q].astype(F32) for k in range(ranks)])
         for k in range(ranks):
             pieces[q, k] = total[:, k * sep : (k + 1) * sep]
         child_out[q] = pieces[q, rank]
@@ -490,13 +513,14 @@
     drain(p2_recv.at[pl.ds(0, group - 1)], send_sems.at[3])
     drain(p3_recv.at[pl.ds(0, n_col - 1)], send_sems.at[4])
     drain(pass_buf.at[pl.ds(0, (rows_all - 1) * n_col)], send_sems.at[5])
-    drain(tile_recv.at[pl.ds(0, n_col - 1)], send_sems.at[6])
-    drain(p4_recv.at[pl.ds(0, n_col - 1)], send_sems.at[7])
-    drain(p5_recv.at[pl.ds(0, everyone - 1)], send_sems.at[8])
-    drain(sr_recv.at[pl.ds(0, rows_all - 1)], send_sems.at[9])
-    drain(kn_recv.at[pl.ds(0, n_col - 1)], send_sems.at[10])
-    drain(p7_recv.at[pl.ds(0, group - 1)], send_sems.at[11])
-    drain(p8_recv.at[pl.ds(0, group - 1)], send_sems.at[12])
+    drain(fw_recv.at[pl.ds(0, n_col - 1)], send_sems.at[6])
+    drain(p5_recv.at[pl.ds(0, rows_all - 1)], send_sems.at[7])
+    drain(sr_recv.at[pl.ds(0, rows_all - 1)], send_sems.at[8])
+    drain(p7_recv.at[pl.ds(0, ranks - 1)], send_sems.at[9])
+    drain(p8_recv.at[pl.ds(0, ranks - 1)], send_sems.at[10])
+    for number, weights in enumerate((child_w, off_w, root_w)):
+        for kind in range(3):
+            drain(weights.at[0], share_sems.at[number, kind])
 
 
 def fused(
@@ -511,7 +535,6 @@
     ranks = n_row * (n_leaf // 2)
     rows_all = n_leaf * n_row
     group = ranks * n_col
-    everyone = rows_all * n_col
     root_width = inv_root.shape[2]
     child_width = inv_child.shape[2]
     sep_blocks = child_width * n_col // BLOCK_ROWS
@@ -549,25 +572,26 @@
         in_specs=[smem] * 4 + [vmem] * 3 + [hbm] * 3,
         out_specs=(vmem, vmem, vmem),
         scratch_shapes=[
-            buffer(*inv_root.shape), buffer(*inv_child.shape), buffer(*off_child.shape),
+            buffer(n_col, *inv_root.shape), buffer(n_col, *inv_child.shape),
+            buffer(n_col, *off_child.shape),
             buffer(group * n_col, panel, BLOCK_ROWS),
             buffer(group, panel, sep),
             buffer(rows_all, n_col, panel, sep),
             buffer(n_col, right, sep), buffer(group, right, sep),
             buffer(n_col, n_col, panel, BLOCK_ROWS), buffer(n_col, n_col, panel, BLOCK_ROWS),
             buffer(n_col, panel, BLOCK_ROWS), buffer(rows_all * n_col, panel, BLOCK_ROWS),
-            buffer(n_col, panel, root_width), buffer(n_col, panel, root_width),
-            buffer(n_col, right, sep), buffer(n_col, n_col, right, sep),
-            buffer(everyone, panel, sep), buffer(everyone, panel, sep),
+            buffer(n_col, panel, sep), buffer(n_col, panel, sep),
+            buffer(rows_all, n_col, panel, sep), buffer(rows_all, n_col, panel, sep),
             buffer(n_col, panel, sep), buffer(rows_all, n_col, panel, sep),
-            buffer(n_col, panel, BLOCK_ROWS), buffer(n_col, n_col, panel, BLOCK_ROWS),
-            buffer(ranks, right, sep), buffer(group, right, sep),
-            buffer(n_col, panel, child_width), buffer(group, panel, child_width),
+            buffer(ranks, n_col, panel, sep), buffer(ranks, n_col, panel, sep),
+            buffer(n_col, panel, child_width), buffer(ranks, n_col, panel, child_width),
             buffer(sep_blocks + root_blocks, panel, BLOCK_ROWS),
             pltpu.VMEM((n_col, ranks, panel, sep), F32),
             pltpu.SemaphoreType.DMA((3,)),
-            pltpu.SemaphoreType.DMA((13,)),
-            pltpu.SemaphoreType.DMA((13,)),
+            pltpu.SemaphoreType.DMA((11,)),
+            pltpu.SemaphoreType.DMA((11,)),
+            pltpu.SemaphoreType.DMA((3, 3)),
+            pltpu.SemaphoreType.DMA((3, 3)),
         ],
         compiler_params=pltpu.CompilerParams(
             collective_id=0, has_side_effects=True, vmem_limit_bytes=32 * 1024 * 1024

time: 66.3 us -> 61.4 us (0.926)
  Pallas kernels: 60.3 us -> 55.4 us
    pallas_call x1, Pallas kernels: 60.3 us -> 55.4 us  [fused(): pl.pallas_call(functools.partial(solve_kernel, (n_leaf, n_row, n_col)), o...]
where the time goes in v2:
time: 61.4 us; the launch traced here: 61.2 us
  Pallas kernels  55.4 us (90%)
  local copies, waits for them, and re-layouts  4.71 us (8%)
  between operations  0.73 us (1%)
    pallas_call x1, Pallas kernels, fused(): pl.pallas_call(functools.partial(solve_kernel, (n_leaf, n_row, n_col)), o...  55.4 us
    unnamed x20, local copies, waits for them, and re-layouts  3.78 us

profile of v2, /device:TPU:0, one launch (start us, length us, event | category | flops | bytes accessed | tf_op | source)
XLA Modules:
  0.0 61.2 jit_solution(8425489282361954753)
XLA Ops:
  0.7 0.0 copy-start.3
  0.7 0.7 %copy-done.3 = s32[2,16]{1,0:T(2,128)S(1)} copy-done((s32[2,16]{1,0:T(2,128)S(1)}, s32[2,16]{1,0:T(2,128)}, u32[]{:S(2)}) %copy-start.3) | copy-done | bytes 152
  1.3 0.0 copy-start.4
  1.3 0.1 select_reduce_fusion
  1.4 0.1 compare_select_fusion.1.root_table
  1.5 0.5 copy-done.4
  2.0 0.1 select_reduce_fusion.1
  2.1 0.1 add_select_fusion.sub_table
  2.2 0.1 reshape.44
  2.3 0.0 copy-start.5
  2.3 0.0 copy-start
  2.3 0.0 copy-start.1
  2.3 0.0 copy-start.2
  2.3 0.8 %gather_fusion = s32[32]{0:T(128)S(1)} fusion(s32[4,16]{1,0:T(4,128)S(1)} %bitcast.19, s32[32]{0:T(128)S(1)} %reshape.44), kind=kCustom, calls=%fused_computation | custom fusion | bytes 512 | tf_op jit(solution)/shard_map/jit(take_along_axis)/gather | solution.py:555
  3.1 0.1 reshape.47
  3.2 0.0 copy-done.5
  3.2 0.0 copy-start.6
  3.2 0.0 copy-start.7
  3.2 0.7 %copy-done.6 = bf16[16,4,96]{2,1,0:T(4,128)(2,1)S(1)} copy-done((bf16[16,4,96]{2,1,0:T(4,128)(2,1)S(1)}, bf16[16,4,96]{2,1,0:T(4,128)(2,1)}, u32[]{:S(2)}) %copy-start.6) | copy-done | bytes 12312
  3.9 0.0 copy-done.7
  3.9 0.0 copy-done
  3.9 0.0 copy-done.1
  3.9 0.0 copy-done.2
  3.9 55.4 %shard_map.103 = (f32[4,16,96]{2,1,0:T(8,128)S(1)}, f32[4,16,96]{2,1,0:T(8,128)S(1)}, bf16[4,16,128]{2,1,0:T(8,128)(2,1)S(1)}) custom-call(s32[4,28]{1,0:T(4,128)S(1)} %add_select_fusion.sub_table, s32[2,24]{1,0:T(2,128)S(1)} %compare_select_fusion.1.root_table, s32[4,8]{1,0:T(4,128)S(1)} %compare_select_fusion.leaf_table, s32[2,16]{1,0:T(2,128)S(1)} %copy-done.3, ...), custom_call_target="tpu_custom_call" | custom-call | tf_op jit(solution)/shard_map/pallas_call | solution.py:565
  59.3 0.6 %copy.26 = f32[16,4,96]{2,1,0:T(4,128)} copy(f32[16,4,96]{2,0,1:T(8,128)S(1)} %bitcast.17) | data formatting | bytes 49152
  60.0 0.6 %copy.27 = f32[16,4,96]{2,1,0:T(4,128)} copy(f32[16,4,96]{2,0,1:T(8,128)S(1)} %bitcast.16) | data formatting | bytes 49152
  60.6 0.6 copy.28
  (9 shorter events, 0.1 us)
Async XLA Ops:
  0.7 0.7 %copy-start.3 = (s32[2,16]{1,0:T(2,128)S(1)}, s32[2,16]{1,0:T(2,128)}, u32[]{:S(2)}) copy-start(s32[2,16]{1,0:T(2,128)} %child_map.1) | copy-start | bytes 388
  1.3 0.7 %copy-start.4 = (s32[4,8]{1,0:T(4,128)S(1)}, s32[4,8]{1,0:T(4,128)}, u32[]{:S(2)}) copy-start(s32[4,8]{1,0:T(4,128)} %param.15) | copy-start | bytes 388
  2.3 0.9 %copy-start.5 = (bf16[16,4,128]{2,1,0:T(4,128)(2,1)S(1)}, bf16[16,4,128]{2,1,0:T(4,128)(2,1)}, u32[]{:S(2)}) copy-start(bf16[16,4,128]{2,1,0:T(4,128)(2,1)} %param.10) | copy-start | bytes 49156
  2.3 1.6 %copy-start = (bf16[4,96,768]{2,1,0:T(8,128)(2,1)S(1)}, bf16[4,96,768]{2,1,0:T(8,128)(2,1)}, u32[]{:S(2)}) copy-start(bf16[4,96,768]{2,1,0:T(8,128)(2,1)} %root_hbm.1) | copy-start | bytes 1769476
  2.3 1.6 %copy-start.1 = (bf16[4,128,384]{2,1,0:T(8,128)(2,1)S(1)}, bf16[4,128,384]{2,1,0:T(8,128)(2,1)}, u32[]{:S(2)}) copy-start(bf16[4,128,384]{2,1,0:T(8,128)(2,1)} %off_hbm.1) | copy-start | bytes 1179652
  2.3 1.6 %copy-start.2 = (bf16[4,96,384]{2,1,0:T(8,128)(2,1)S(1)}, bf16[4,96,384]{2,1,0:T(8,128)(2,1)}, u32[]{:S(2)}) copy-start(bf16[4,96,384]{2,1,0:T(8,128)(2,1)} %child_hbm.1) | copy-start | bytes 884740
  3.2 0.7 %copy-start.6 = (bf16[16,4,96]{2,1,0:T(4,128)(2,1)S(1)}, bf16[16,4,96]{2,1,0:T(4,128)(2,1)}, u32[]{:S(2)}) copy-start(bf16[16,4,96]{2,1,0:T(4,128)(2,1)} %param.8) | copy-start | bytes 36868
  3.2 0.7 %copy-start.7 = (bf16[16,4,96]{2,1,0:T(4,128)(2,1)S(1)}, bf16[16,4,96]{2,1,0:T(4,128)(2,1)}, u32[]{:S(2)}) copy-start(bf16[16,4,96]{2,1,0:T(4,128)(2,1)} %param.9) | copy-start | bytes 36868

commit v3 on v2

--- a/solution.py
+++ b/solution.py
@@ -225,11 +225,6 @@
 BF16 = jnp.bfloat16
 
 
-def inverse_table(block_map, blocks_total, places):
-    hit = block_map[..., None] == jnp.arange(blocks_total, dtype=jnp.int32)
-    return jnp.sum(jnp.where(hit, places[:, None] + 1, 0), axis=-2, dtype=jnp.int32) - 1
-
-
 def add_up(terms):
     total = terms[0]
     for term in terms[1:]:
@@ -239,11 +234,11 @@
 
 def solve_kernel(
     dims,
-    sub_table, root_table, leaf_table, child_map,
+    child_map, subtree_map,
     sub_in, rc_in, rr_in, root_hbm, child_hbm, off_hbm,
     root_out, child_out, leaf_out,
     root_w, child_w, off_w,
-    sub_buf, rc_buf, rr_buf,
+    p1_send, p1_recv, tail_send, tail_recv, rr_buf,
     p2_send, p2_recv, p3_send, p3_recv, pass_send, pass_buf,
     fw_send, fw_recv, p5_send, p5_recv,
     sr_send, sr_recv, p7_send, p7_recv, p8_send, p8_recv,
@@ -312,28 +307,48 @@
 
     pair = c + 1 - 2 * lax.rem(c, 2)
     across = lax.rem(c + 2, n_col)
-
-    def hand(weights, slot, number, kind, c2):
+    far = lax.rem(pair + 2, n_col)
+
+    def tiles_of(number, c2, body, rows=(3, 2, 1, 0)):
+        for q in rows:
+            if number == 1:
+                body(q)
+            else:
+                pl.when(q >= c2)(functools.partial(body, q))
+
+    def hand(weights, slot, q, number, kind, c2):
         pltpu.make_async_remote_copy(
-            src_ref=weights.at[slot],
-            dst_ref=weights.at[slot],
-            send_sem=share_sems.at[number, kind],
-            recv_sem=shared_sems.at[number, kind],
+            src_ref=weights.at[slot, q],
+            dst_ref=weights.at[slot, q],
+            send_sem=share_sems.at[number, kind, q],
+            recv_sem=shared_sems.at[number, kind, q],
             device_id=at_row(r, c2),
             device_id_type=pl.DeviceIdType.MESH,
         ).start()
 
     def share(weights, number):
-        hand(weights, c, number, 0, across)
-        hand(weights, c, number, 1, pair)
-
-    def relay(weights, number):
-        drain(weights.at[across], shared_sems.at[number, 0])
-        hand(weights, across, number, 2, pair)
+        tiles_of(number, c, lambda q: hand(weights, c, q, number, 0, across))
+        tiles_of(number, c, lambda q: hand(weights, c, q, number, 1, pair))
+
+    def relay(weights, number, rows=(3, 2, 1, 0)):
+        def pass_on(q):
+            drain(weights.at[across, q], shared_sems.at[number, 0, q])
+            hand(weights, across, q, number, 2, pair)
+
+        tiles_of(number, across, pass_on, rows)
 
     def settle(weights, number):
-        drain(weights.at[0], shared_sems.at[number, 1])
-        drain(weights.at[0], shared_sems.at[number, 2])
+        tiles_of(number, pair, lambda q: drain(weights.at[0, q], shared_sems.at[number, 1, q]))
+        tiles_of(number, far, lambda q: drain(weights.at[0, q], shared_sems.at[number, 2, q]))
+
+    def conclude(weights, number):
+        for kind, slot in enumerate((c, c, across)):
+            tiles_of(
+                number, slot, lambda q: drain(weights.at[0, q], share_sems.at[number, kind, q])
+            )
+
+    def lower(weights, c2):
+        return weights[c2, c2:].reshape(-1, weights.shape[3])
 
     def flat(weights, c2):
         return weights[c2].reshape(-1, weights.shape[3])
@@ -341,49 +356,60 @@
     each(group, gid, lambda g2: greet(at_group(g2)))
     for k in range(ranks):
         greet(at_row((1 - front) * ranks + k, c))
+
+    update = [sub_in[q].astype(F32) for q in range(n_col)]
+    targets = [subtree_map[leaf, q * n_row + row] for q in range(n_col)]
+
+    def own_block(block):
+        return add_up(
+            [
+                jnp.where(target == block, value, jnp.zeros_like(value))
+                for target, value in zip(targets, update)
+            ]
+        )
+
+    for c2 in range(n_col):
+        rhs = rc_in[c2].astype(F32)
+        rhs = jnp.concatenate(
+            [jnp.where(rank == k, rhs, jnp.zeros_like(rhs)) for k in range(ranks)], 1
+        )
+        placed = jnp.concatenate(
+            [own_block(c2 * child_tile_blocks + b) for b in range(child_tile_blocks)], 1
+        )
+        p1_send[c2] = (rhs + placed).astype(BF16)
+    for k in range(ranks):
+        for q in range(n_col):
+            tail_send[k, q] = own_block(sep_blocks + q * ranks + k).astype(BF16)
     pl.semaphore_wait(barrier, group - 1 + ranks)
 
-    each(group, gid, lambda g2: push(rc_in.at[lax.div(g2, ranks)], rc_buf.at[gid], 1, at_group(g2)))
-    each(group, gid, lambda g2: push(sub_in, sub_buf.at[pl.ds(gid * n_col, n_col)], 0, at_group(g2)))
+    each(group, gid, lambda g2: push(p1_send.at[lax.div(g2, ranks)], p1_recv.at[gid], 0, at_group(g2)))
+
+    def each_rank(body):
+        each(ranks, rank, lambda k: body(k, at_row(front * ranks + k, c)))
+
+    each_rank(lambda k, device: push(tail_send.at[k], tail_recv.at[rank], 1, device))
     each(rows_all, r, lambda r2: push(rr_in, rr_buf.at[r], 2, at_row(r2, c)))
-    sub_buf[pl.ds(gid * n_col, n_col)] = sub_in[...]
-    rc_buf[gid] = rc_in[c]
+    p1_recv[gid] = p1_send[c]
+    tail_recv[rank] = tail_send[rank]
     rr_buf[r] = rr_in[...]
     loads[2].wait()
     share(root_w, 2)
     loads[0].wait()
-    drain(rc_buf.at[pl.ds(0, group - 1)], recv_sems.at[1])
-    drain(sub_buf.at[pl.ds(0, (group - 1) * n_col)], recv_sems.at[0])
-
-    def placed(p, block):
-        total = None
-        for h in range(2):
-            place = sub_table[2 * front + h, block]
-            value = sub_buf[p * ranks * n_col + jnp.maximum(place, 0)].astype(F32)
-            value = jnp.where(place >= 0, value, jnp.zeros_like(value))
-            total = value if total is None else total + value
-        return total
-
-    def rows_of(values):
-        return jnp.concatenate(values, 0)
-
+    drain(p1_recv.at[pl.ds(0, group - 1)], recv_sems.at[0])
     x = jnp.concatenate(
-        [rows_of([rc_buf[p * ranks + k] for p in range(n_col)]).astype(F32) for k in range(ranks)], 1
-    )
-    x = x + jnp.concatenate(
         [
-            rows_of([placed(p, c * child_tile_blocks + b) for p in range(n_col)])
-            for b in range(child_tile_blocks)
+            add_up([p1_recv[p * ranks + k].astype(F32) for k in range(ranks)])
+            for p in range(n_col)
         ],
-        1,
-    )
-    x = x.astype(BF16)
+        0,
+    ).astype(BF16)
     for q in range(n_col):
         p2_send[q] = contract(x, child_w[c, q], 1, 1).astype(BF16)
 
     each(group, gid, lambda g2: push(p2_send.at[lax.div(g2, ranks)], p2_recv.at[gid], 3, at_group(g2)))
     p2_recv[gid] = p2_send[c]
-    tail = [placed(c, sep_blocks + q * ranks + rank) for q in range(n_col)]
+    drain(tail_recv.at[pl.ds(0, ranks - 1)], recv_sems.at[1])
+    tail = [add_up([tail_recv[k, q].astype(F32) for k in range(ranks)]) for q in range(n_col)]
     loads[1].wait()
     drain(p2_recv.at[pl.ds(0, group - 1)], recv_sems.at[3])
     forward = [
@@ -402,7 +428,6 @@
     fw_send[...] = own.astype(BF16).reshape(fw_send.shape)
     each(n_col, c, lambda c2: push(fw_send.at[c2], fw_recv.at[c], 6, at_row(r, c2)))
     fw_recv[c] = fw_send[c]
-    share(off_w, 1)
     drain(p3_recv.at[pl.ds(0, n_col - 1)], recv_sems.at[4])
     for q in range(n_col):
         total = add_up([p3_recv[c2, q].astype(F32) for c2 in range(n_col)])
@@ -410,17 +435,31 @@
 
     each(rows_all, r, lambda r2: push(pass_send, pass_buf.at[pl.ds(r * n_col, n_col)], 5, at_row(r2, c)))
     pass_buf[pl.ds(r * n_col, n_col)] = pass_send[...]
-    relay(root_w, 2)
+    relay(root_w, 2, (3, 2, 1, 0))
+    share(off_w, 1)
+    targets = [[child_map[f, j] for j in range(child_map.shape[1])] for f in range(2)]
+
+    def place_of(f, block):
+        place = -1
+        for j, target in enumerate(targets[f]):
+            source = (f * ranks + j % ranks) * n_col + j // ranks
+            place = jnp.where(target == block, source, place)
+        return place
+
+    places = [[place_of(f, b) for f in range(2)] for b in range(root_tile_blocks * n_col)]
     drain(rr_buf.at[pl.ds(0, rows_all - 1)], recv_sems.at[2])
     x = jnp.concatenate(
         [rr_buf[k].reshape(right, sep).astype(F32) for k in range(rows_all)], 1
     )
     drain(pass_buf.at[pl.ds(0, (rows_all - 1) * n_col)], recv_sems.at[5])
 
+    def rows_of(values):
+        return jnp.concatenate(values, 0)
+
     def passed(block):
         total = None
         for f in range(2):
-            place = root_table[f, block]
+            place = places[block][f]
             value = pass_buf[jnp.maximum(place, 0)].astype(F32)
             value = jnp.where(place >= 0, value, jnp.zeros_like(value))
             total = value if total is None else total + value
@@ -435,14 +474,15 @@
     )
     x = x.astype(BF16)
     settle(root_w, 2)
-    root_forward = add_up(
-        [
-            contract(x[c2 * panel : (c2 + 1) * panel], flat(root_w, c2), 1, 1)
-            for c2 in range(n_col)
-        ]
-    ).astype(BF16)
+    terms = []
     for c2 in range(n_col):
-        total = contract(root_forward, flat(root_w, c2), 1, 0)
+        term = contract(x[c2 * panel : (c2 + 1) * panel], lower(root_w, c2), 1, 1)
+        if c2 > 0:
+            term = jnp.concatenate([jnp.zeros((panel, c2 * sep), F32), term], 1)
+        terms.append(term)
+    root_forward = add_up(terms)
+    for c2 in range(n_col):
+        total = contract(root_forward[:, c2 * sep :].astype(BF16), lower(root_w, c2), 1, 0)
         for r2 in range(rows_all):
             p5_send[r2, c2] = total[:, r2 * sep : (r2 + 1) * sep].astype(BF16)
 
@@ -476,9 +516,6 @@
         for k in range(ranks):
             p7_send[k, c2] = total[:, k * sep : (k + 1) * sep].astype(BF16)
 
-    def each_rank(body):
-        each(ranks, rank, lambda k: body(k, at_row(front * ranks + k, c)))
-
     each_rank(lambda k, device: push(p7_send.at[k], p7_recv.at[rank], 9, device))
     p7_recv[rank] = p7_send[rank]
     relay(child_w, 0)
@@ -488,10 +525,11 @@
     for q in range(n_col):
         total = add_up([p7_recv[k, q].astype(F32) for k in range(ranks)])
         back.append(fw_recv[q].astype(F32) - total)
-    back = jnp.concatenate(back, 1).astype(BF16)
+    back = jnp.concatenate(back, 1)
     settle(child_w, 0)
     for c2 in range(n_col):
-        p8_send[c2] = contract(back, flat(child_w, c2), 1, 0).astype(BF16)
+        total = contract(back[:, c2 * sep :].astype(BF16), lower(child_w, c2), 1, 0)
+        p8_send[c2] = total.astype(BF16)
 
     each_rank(lambda k, device: push(p8_send, p8_recv.at[rank], 10, device))
     p8_recv[rank] = p8_send[...]
@@ -505,10 +543,12 @@
         for b in range(child_tile_blocks):
             blocks[q * child_tile_blocks + b] = total[:, b * BLOCK_ROWS : (b + 1) * BLOCK_ROWS]
     for q in range(n_col):
-        leaf_out[q] = blocks[leaf_table[leaf, q * n_row + row]]
-
-    drain(rc_buf.at[pl.ds(0, group - 1)], send_sems.at[1])
-    drain(sub_buf.at[pl.ds(0, (group - 1) * n_col)], send_sems.at[0])
+        block = subtree_map[leaf, q * n_row + row]
+        known_block = sep_blocks + child_map[front, jnp.maximum(block - sep_blocks, 0)]
+        leaf_out[q] = blocks[jnp.where(block < sep_blocks, block, known_block)]
+
+    drain(p1_recv.at[pl.ds(0, group - 1)], send_sems.at[0])
+    drain(tail_recv.at[pl.ds(0, ranks - 1)], send_sems.at[1])
     drain(rr_buf.at[pl.ds(0, rows_all - 1)], send_sems.at[2])
     drain(p2_recv.at[pl.ds(0, group - 1)], send_sems.at[3])
     drain(p3_recv.at[pl.ds(0, n_col - 1)], send_sems.at[4])
@@ -519,8 +559,7 @@
     drain(p7_recv.at[pl.ds(0, ranks - 1)], send_sems.at[9])
     drain(p8_recv.at[pl.ds(0, ranks - 1)], send_sems.at[10])
     for number, weights in enumerate((child_w, off_w, root_w)):
-        for kind in range(3):
-            drain(weights.at[0], share_sems.at[number, kind])
+        conclude(weights, number)
 
 
 def fused(
@@ -539,21 +578,6 @@
     child_width = inv_child.shape[2]
     sep_blocks = child_width * n_col // BLOCK_ROWS
     root_blocks = root_width * n_col // BLOCK_ROWS
-    sub_count = subtree_map.shape[1]
-    upd_count = child_map.shape[1]
-
-    number = jnp.arange(sub_count, dtype=jnp.int32)
-    half = (jnp.arange(4, dtype=jnp.int32) % 2)[:, None]
-    within = (number % n_row) * n_col + number // n_row
-    sub_table = inverse_table(subtree_map, sep_blocks + upd_count, within)
-    sub_table = jnp.where(sub_table >= 0, sub_table + half * n_row * n_col, -1)
-    number = jnp.arange(upd_count, dtype=jnp.int32)
-    root_table = inverse_table(child_map, root_blocks, (number % ranks) * n_col + number // ranks)
-    child = jnp.arange(2, dtype=jnp.int32)[:, None]
-    root_table = jnp.where(root_table >= 0, root_table + child * ranks * n_col, -1)
-    beyond = jnp.clip(subtree_map - sep_blocks, 0)
-    known = jnp.take_along_axis(jnp.repeat(child_map, 2, axis=0), beyond, axis=1)
-    leaf_table = jnp.where(subtree_map < sep_blocks, subtree_map, sep_blocks + known)
 
     def turn(array):
         return array.transpose(1, 0, 2)
@@ -569,13 +593,13 @@
             jax.ShapeDtypeStruct((n_col, panel, sep), F32),
             jax.ShapeDtypeStruct((n_col, panel, BLOCK_ROWS), BF16),
         ),
-        in_specs=[smem] * 4 + [vmem] * 3 + [hbm] * 3,
+        in_specs=[smem] * 2 + [vmem] * 3 + [hbm] * 3,
         out_specs=(vmem, vmem, vmem),
         scratch_shapes=[
             buffer(n_col, *inv_root.shape), buffer(n_col, *inv_child.shape),
             buffer(n_col, *off_child.shape),
-            buffer(group * n_col, panel, BLOCK_ROWS),
-            buffer(group, panel, sep),
+            buffer(n_col, panel, child_width), buffer(group, panel, child_width),
+            buffer(ranks, n_col, panel, BLOCK_ROWS), buffer(ranks, n_col, panel, BLOCK_ROWS),
             buffer(rows_all, n_col, panel, sep),
             buffer(n_col, right, sep), buffer(group, right, sep),
             buffer(n_col, n_col, panel, BLOCK_ROWS), buffer(n_col, n_col, panel, BLOCK_ROWS),
@@ -590,14 +614,14 @@
             pltpu.SemaphoreType.DMA((3,)),
             pltpu.SemaphoreType.DMA((11,)),
             pltpu.SemaphoreType.DMA((11,)),
-            pltpu.SemaphoreType.DMA((3, 3)),
-            pltpu.SemaphoreType.DMA((3, 3)),
+            pltpu.SemaphoreType.DMA((3, 3, 4)),
+            pltpu.SemaphoreType.DMA((3, 3, 4)),
         ],
         compiler_params=pltpu.CompilerParams(
             collective_id=0, has_side_effects=True, vmem_limit_bytes=32 * 1024 * 1024
         ),
     )(
-        sub_table, root_table, leaf_table, child_map,
+        child_map, subtree_map,
         turn(subtree_update), turn(rhs_child), turn(rhs_root), inv_root, inv_child, off_child,
     )
     return tuple(turn(out) for out in outs)

time: 61.4 us -> 60.8 us (level)
  Pallas kernels: 55.4 us -> 53.5 us
  local copies, waits for them, and re-layouts: 4.71 us -> 6.32 us
    unnamed x20 -> x18, local copies, waits for them, and re-layouts: 3.78 us -> 6.31 us
    pallas_call x1, Pallas kernels: 55.4 us -> 53.5 us  [fused(): pl.pallas_call(functools.partial(solve_kernel, (n_leaf, n_row, n_col)), o...]
    gather x3 -> x0, local copies, waits for them, and re-layouts: 0.92 us -> none  [fused(): jnp.take_along_axis(jnp.repeat(child_map, 2, axis=0), beyond, axis=1)]
where the time goes in v3:
time: 60.8 us; the launch traced here: 60.5 us
  Pallas kernels  53.5 us (88%)
  local copies, waits for them, and re-layouts  6.32 us (10%)
  between operations  0.69 us (1%)
    pallas_call x1, Pallas kernels, fused(): pl.pallas_call(functools.partial(solve_kernel, (n_leaf, n_row, n_col)), o...  53.5 us
    unnamed x18, local copies, waits for them, and re-layouts  6.31 us

profile of v3, /device:TPU:0, one launch (start us, length us, event | category | flops | bytes accessed | tf_op | source)
XLA Modules:
  0.0 60.5 jit_solution(8802812155916332377)
XLA Ops:
  0.6 0.0 copy-start.6
  0.6 0.0 copy-start.5
  0.7 0.7 %copy.20 = bf16[16,4,128]{2,0,1:T(8,128)(2,1)S(1)} copy(bf16[16,4,128]{2,1,0:T(4,128)(2,1)} %param.10) | data formatting | bytes 32768 | tf_op args[2]
  1.4 0.0 copy-done.6
  1.4 0.0 copy-done.5
  1.4 0.0 copy-start.3
  1.4 0.0 copy-start.4
  1.4 0.7 %copy-done.3 = s32[4,8]{1,0:T(4,128)S(1)} copy-done((s32[4,8]{1,0:T(4,128)S(1)}, s32[4,8]{1,0:T(4,128)}, u32[]{:S(2)}) %copy-start.3) | copy-done | bytes 152
  2.1 0.0 copy-done.4
  2.1 0.0 copy-start
  2.1 1.1 %copy-done = bf16[4,96,768]{2,1,0:T(8,128)(2,1)S(1)} copy-done((bf16[4,96,768]{2,1,0:T(8,128)(2,1)S(1)}, bf16[4,96,768]{2,1,0:T(8,128)(2,1)}, u32[]{:S(2)}) %copy-start) | copy-done | bytes 589848
  3.2 0.0 copy-start.1
  3.2 1.0 %copy-done.1 = bf16[4,128,384]{2,1,0:T(8,128)(2,1)S(1)} copy-done((bf16[4,128,384]{2,1,0:T(8,128)(2,1)S(1)}, bf16[4,128,384]{2,1,0:T(8,128)(2,1)}, u32[]{:S(2)}) %copy-start.1) | copy-done | bytes 393240
  4.2 0.0 copy-start.2
  4.2 1.0 %copy-done.2 = bf16[4,96,384]{2,1,0:T(8,128)(2,1)S(1)} copy-done((bf16[4,96,384]{2,1,0:T(8,128)(2,1)S(1)}, bf16[4,96,384]{2,1,0:T(8,128)(2,1)}, u32[]{:S(2)}) %copy-start.2) | copy-done | bytes 294936
  5.1 53.5 %shard_map.103 = (f32[4,16,96]{2,1,0:T(8,128)S(1)}, f32[4,16,96]{2,1,0:T(8,128)S(1)}, bf16[4,16,128]{2,1,0:T(8,128)(2,1)S(1)}) custom-call(s32[2,16]{1,0:T(2,128)S(1)} %copy-done.4, s32[4,8]{1,0:T(4,128)S(1)} %copy-done.3, bf16[4,16,128]{2,1,0:T(8,128)(2,1)S(1)} %bitcast.10, bf16[4,16,96]{2,1,0:T(8,128)(2,1)S(1)} %get-tuple-element.13.rc_in, ...), custom_call_target="tpu_custom_call" | custom-call | tf_op jit(solution)/shard_map/pallas_call | solution.py:589
  58.6 0.6 %copy.14 = f32[16,4,96]{2,1,0:T(4,128)} copy(f32[16,4,96]{2,0,1:T(8,128)S(1)} %bitcast.12) | data formatting | bytes 49152
  59.2 0.6 %copy.15 = f32[16,4,96]{2,1,0:T(4,128)} copy(f32[16,4,96]{2,0,1:T(8,128)S(1)} %bitcast.11) | data formatting | bytes 49152
  59.9 0.6 %copy.16 = bf16[16,4,128]{2,1,0:T(4,128)(2,1)} copy(bf16[16,4,128]{2,0,1:T(8,128)(2,1)S(1)} %bitcast.13) | data formatting | bytes 32768
  (1 shorter events, 0.0 us)
Async XLA Ops:
  0.6 0.8 %copy-start.6 = (bf16[16,4,96]{2,1,0:T(4,128)(2,1)S(1)}, bf16[16,4,96]{2,1,0:T(4,128)(2,1)}, u32[]{:S(2)}) copy-start(bf16[16,4,96]{2,1,0:T(4,128)(2,1)} %param.9) | copy-start | bytes 36868
  0.6 0.7 %copy-start.5 = (bf16[16,4,96]{2,1,0:T(4,128)(2,1)S(1)}, bf16[16,4,96]{2,1,0:T(4,128)(2,1)}, u32[]{:S(2)}) copy-start(bf16[16,4,96]{2,1,0:T(4,128)(2,1)} %param.8) | copy-start | bytes 36868
  1.4 0.7 %copy-start.3 = (s32[4,8]{1,0:T(4,128)S(1)}, s32[4,8]{1,0:T(4,128)}, u32[]{:S(2)}) copy-start(s32[4,8]{1,0:T(4,128)} %subtree_map.1) | copy-start | bytes 388
  1.4 0.7 %copy-start.4 = (s32[2,16]{1,0:T(2,128)S(1)}, s32[2,16]{1,0:T(2,128)}, u32[]{:S(2)}) copy-start(s32[2,16]{1,0:T(2,128)} %child_map.1) | copy-start | bytes 388
  2.1 1.1 %copy-start = (bf16[4,96,768]{2,1,0:T(8,128)(2,1)S(1)}, bf16[4,96,768]{2,1,0:T(8,128)(2,1)}, u32[]{:S(2)}) copy-start(bf16[4,96,768]{2,1,0:T(8,128)(2,1)} %root_hbm.1) | copy-start | bytes 1769476
  3.2 1.0 %copy-start.1 = (bf16[4,128,384]{2,1,0:T(8,128)(2,1)S(1)}, bf16[4,128,384]{2,1,0:T(8,128)(2,1)}, u32[]{:S(2)}) copy-start(bf16[4,128,384]{2,1,0:T(8,128)(2,1)} %off_hbm.1) | copy-start | bytes 1179652
  4.2 1.0 %copy-start.2 = (bf16[4,96,384]{2,1,0:T(8,128)(2,1)S(1)}, bf16[4,96,384]{2,1,0:T(8,128)(2,1)}, u32[]{:S(2)}) copy-start(bf16[4,96,384]{2,1,0:T(8,128)(2,1)} %child_hbm.1) | copy-start | bytes 884740
